TPU v7x, 32 devices: a whole 2x2x4 slice. The times are simulated.
32 devices in a mesh: row: 8 (over z, y), col: 4 (over x, core).
Axes of the slice: x: 2, y: 2, z: 4, core: 2. Of those that a mesh axis runs over, the one named last changes fastest.
Arguments:
- feature: bfloat16 [128, 1024, 192], P('row', 'col'), may hold values from -6 to 6
- mask: int32 [128, 1024], P('row', 'col'), may hold values from 0 to 1, as said below
- dw_weight: float32 [7, 7, 192], replicated, may hold values from -1.75 to 1.75
- dw_bias: float32 [192], replicated, may hold values from -3 to 3
- ln_gain: float32 [192], replicated, may hold values from 0.25 to 1.75
- ln_bias: float32 [192], replicated, may hold values from -2.5 to 2.5
- w_in: bfloat16 [192, 768], replicated, may hold values from -0.4375 to 0.4375
- b_in: float32 [768], replicated, may hold values from -3 to 3
- w_out: bfloat16 [768, 192], replicated, may hold values from -0.3125 to 0.3125
- b_out: float32 [192], replicated, may hold values from -2.5 to 2.5
- layer_scale: float32 [192], replicated, may hold values from 0.2 to 1.5
- w_key: bfloat16 [192, 192], replicated, may hold values from -0.4375 to 0.4375
- w_value: bfloat16 [192, 192], replicated, may hold values from -0.4375 to 0.4375
- queries: bfloat16 [512, 192], replicated, may hold values from -160 to 160
- w_proj: bfloat16 [192, 192], replicated, may hold values from -0.4375 to 0.4375
Outputs:
- block_out: bfloat16 [128, 1024, 192], P('row', 'col')
- pooled_out: float32 [512, 192], replicated
Inputs may be any that keep to these rules, and one draw needn't show every extreme that they name: `mask`: position (0, 0) is tissue; tissue comes in regions, and some devices' blocks hold none.
All inputs are finite; a program needn't handle non-finite values.
Results may differ from a plain program's by a relative error of at most 0.015.
Values may be sent and summed in bfloat16 or wider, within the bound.
A program may use at most 128 MiB of HBM per device.

v0:
```python
import jax
import jax.numpy as jnp
from jax import lax
from jax.sharding import PartitionSpec as P

NH = 8


def padded_2(value, sides, width):
    for axis, dim in sides:
        count, length = (lax.axis_size(axis), value.shape[dim])
        up = [(i, (i + 1) % count) for i in range(count - 1)]
        down = [(j, i) for i, j in up]
        last = lax.slice_in_dim(value, length - width, length, axis=dim)
        initial = lax.slice_in_dim(value, 0, width, axis=dim)
        before = lax.ppermute(last, axis, up)
        after = lax.ppermute(initial, axis, down)
        value = jnp.concatenate([before, value, after], axis=dim)
    return value


def merged_2(value, axis, join):
    pieces = jax.tree.map(lambda part: lax.all_gather(part, axis), value)
    head = jax.tree.map(lambda part: part[0], pieces)
    tail = jax.tree.map(lambda part: part[1:], pieces)
    total, _ = lax.scan(lambda total, slab: (join(total, slab), None), head, tail)
    return total


def pool_group(running, key_group, value_group, mask_group, query_heads, heads, head_size):
    top, total, accum = running
    key_tiles = key_group.reshape(-1, 128, heads, head_size)
    value_tiles = value_group.reshape(-1, 128, heads, head_size)
    tissue = mask_group.reshape(-1, 128) > 0
    scores = jnp.einsum(
        "qhd,tphd->thqp", query_heads, key_tiles, preferred_element_type=jnp.float32
    ) * (1.0 / head_size**0.5)
    scores = jnp.where(tissue[:, None, None, :], scores, -jnp.inf)
    tile_top = jnp.max(scores, axis=-1)
    safe_top = jnp.where(jnp.isfinite(tile_top), tile_top, 0.0)
    weights = jnp.where(
        tissue[:, None, None, :], jnp.exp(scores - safe_top[..., None]), 0.0
    ).astype(jnp.bfloat16)
    tile_total = jnp.sum(weights.astype(jnp.float32), axis=-1)
    tile_accum = jnp.einsum(
        "thqp,tphd->thqd", weights, value_tiles, preferred_element_type=jnp.float32
    )
    new_top = jnp.maximum(top, jnp.max(tile_top, axis=0))
    keep = jnp.exp(top - new_top)
    factor = jnp.exp(tile_top - new_top)
    total = total * keep + jnp.sum(factor * tile_total, axis=0)
    accum = accum * keep[..., None] + jnp.sum(factor[..., None] * tile_accum, axis=0)
    return (new_top, total, accum)


def combine_parts(first, second):
    new_top = jnp.maximum(first[0], second[0])
    left = jnp.exp(first[0] - new_top)
    right = jnp.exp(second[0] - new_top)
    total = first[1] * left + second[1] * right
    accum = first[2] * left[..., None] + second[2] * right[..., None]
    return (new_top, total, accum)


def body(
    feature,
    mask,
    dw_weight,
    dw_bias,
    ln_gain,
    ln_bias,
    w_in,
    b_in,
    w_out,
    b_out,
    layer_scale,
    w_key,
    w_value,
    queries,
    w_proj,
):
    local_rows, local_cols, channels = feature.shape
    padded = padded_2(feature, (("row", 0), ("col", 1)), 3)
    conv = jnp.zeros(feature.shape, jnp.float32)
    for offset_row in range(7):
        for offset_col in range(7):
            window = padded[
                offset_row : offset_row + local_rows, offset_col : offset_col + local_cols, :
            ]
            conv = conv + window.astype(jnp.float32) * dw_weight[offset_row, offset_col]
    conv = conv + dw_bias
    positions = local_rows * local_cols
    block_count = positions // 512
    tile_count = positions // 128
    conv_blocks = conv.reshape(block_count, 512, channels)
    center_blocks = feature.reshape(block_count, 512, channels)

    def mlp_block(pieces):
        flat, center_flat = pieces
        average = jnp.mean(flat, axis=-1, keepdims=True)
        spread = jnp.mean((flat - average) ** 2, axis=-1, keepdims=True)
        normed = ((flat - average) * lax.rsqrt(spread + 1e-06) * ln_gain + ln_bias).astype(
            jnp.bfloat16
        )
        inner = jnp.dot(normed, w_in, preferred_element_type=jnp.float32) + b_in
        hidden = jax.nn.gelu(inner, approximate=False).astype(jnp.bfloat16)
        branch = jnp.dot(hidden, w_out, preferred_element_type=jnp.float32) + b_out
        return (center_flat.astype(jnp.float32) + layer_scale * branch).astype(jnp.bfloat16)

    result_blocks = lax.map(mlp_block, (conv_blocks, center_blocks))
    result_flat = result_blocks.reshape(positions, channels)
    keys = jnp.dot(result_flat, w_key, preferred_element_type=jnp.float32).astype(jnp.bfloat16)
    values = jnp.dot(result_flat, w_value, preferred_element_type=jnp.float32).astype(jnp.bfloat16)
    key_tiles = keys.reshape(tile_count, 128, channels)
    value_tiles = values.reshape(tile_count, 128, channels)
    mask_tiles = mask.reshape(tile_count, 128)
    query_count = queries.shape[0]
    heads = NH
    head_size = channels // heads
    query_heads = queries.reshape(query_count, heads, head_size)
    inputs = (
        key_tiles.reshape(block_count, 512, channels),
        value_tiles.reshape(block_count, 512, channels),
        mask_tiles.reshape(block_count, 512),
    )
    start_state = (
        jnp.full((heads, query_count), -1e30, jnp.float32),
        jnp.zeros((heads, query_count), jnp.float32),
        jnp.zeros((heads, query_count, head_size), jnp.float32),
    )

    def advance(running, items):
        updated = pool_group(running, items[0], items[1], items[2], query_heads, heads, head_size)
        return (updated, None)

    local_state, unused = lax.scan(advance, start_state, inputs)
    partial_state = merged_2(local_state, "col", combine_parts)
    merged = merged_2(partial_state, "row", combine_parts)
    pooled = merged[2] / merged[1][..., None]
    pooled = jnp.transpose(pooled, (1, 0, 2)).reshape(query_count, channels).astype(jnp.bfloat16)
    pooled_out = jnp.dot(pooled, w_proj, preferred_element_type=jnp.float32)
    return (result_flat.reshape(local_rows, local_cols, channels), pooled_out)


def solution(mesh):
    return jax.shard_map(
        body,
        mesh=mesh,
        in_specs=(
            P("row", "col", None),
            P("row", "col"),
            P(),
            P(),
            P(),
            P(),
            P(),
            P(),
            P(),
            P(),
            P(),
            P(),
            P(),
            P(),
            P(),
        ),
        out_specs=(P("row", "col", None), P()),
        check_vma=False,
    )
```

profile of v0, /device:TPU:1, one launch (start us, length us, event | category | flops | bytes accessed | tf_op | source)
XLA Modules:
  0.0 355.8 jit_solution(9773038548651617925)
XLA Ops:
  7.2 1.8 fusion.114
  9.1 4.0 %collective-permute-start = (bf16[3,256,192]{1,2,0:T(8,128)(2,1)S(1)}, bf16[3,256,192]{1,2,0:T(8,128)(2,1)S(1)}, u32[]{:S(2)}, u32[]{:S(2)}) collective-permute-start(bf16[3,256,192]{1,2,0:T(8,128)(2,1)S(1)} %get-tuple-element.397), channel_id=1, source_target_pairs={{0,4},{4,8},{8,12},{12,16},{16,20},{20,24},{24,28},{1,5},{5,9},{9,... | collective-permute-start | bytes 884744 | tf_op jit(solution)/shard_map/ppermute | solution.py:16
  15.4 3.2 copy.76
  19.3 5.7 %collective-permute-done = bf16[3,256,192]{1,2,0:T(8,128)(2,1)S(1)} collective-permute-done((bf16[3,256,192]{1,2,0:T(8,128)(2,1)S(1)}, bf16[3,256,192]{1,2,0:T(8,128)(2,1)S(1)}, u32[]{:S(2)}, u32[]{:S(2)}) %collective-permute-start) | collective-permute-done | bytes 294944 | tf_op jit(solution)/shard_map/ppermute | solution.py:16
  27.2 4.6 %collective-permute-start.2 = (bf16[22,3,192]{2,0,1:T(8,128)(2,1)S(1)}, bf16[22,3,192]{2,0,1:T(8,128)(2,1)S(1)}, u32[]{:S(2)}, u32[]{:S(2)}) collective-permute-start(bf16[22,3,192]{2,0,1:T(8,128)(2,1)S(1)} %get-tuple-element.395), channel_id=1, source_target_pairs={{0,1},{1,2},{2,3},{4,5},{5,6},{6,7},{8,9},{9,10},{10,11},{12,13},{... | collective-permute-start | bytes 76040 | tf_op jit(solution)/shard_map/ppermute | solution.py:16
  31.8 1.9 collective-permute-start.3
  34.3 2.1 copy.74
  36.4 3.6 %reshape.70 = bf16[8,512,192]{1,0,2:T(8,128)(2,1)} reshape(bf16[16,256,192]{1,0,2:T(8,128)(2,1)} %copy.74) | data formatting | bytes 3145728 | tf_op jit(solution)/shard_map/reshape | solution.py:96
  40.0 3.1 copy.84
  43.3 7.5 %maximum_maximum_fusion = (bf16[22,259,192]{2,0,1:T(8,128)(2,1)S(1)}, bf16[22,259,192]{2,0,1:T(8,128)(2,1)S(1)}) fusion(bf16[3,256,192]{2,0,1:T(4,128)(2,1)} %copy.77, bf16[16,256,192]{2,0,1:T(8,128)(2,1)S(1)} %copy.76, bf16[3,256,192]{2,0,1:T(4,128)(2,1)S(1)} %copy.75, bf16[22,3,192]{2,0,1:T(8,128)(2,1)S(1)} %collective-permute-done.2, ...), kind=kLoop, calls=%fused_computation.152 | loop fusion | flops 17504256 | bytes 6589440 | tf_op jit(solution)/shard_map/concatenate | solution.py:18
  51.0 34.0 %add_add_fusion = f32[16,256,192]{2,0,1:T(8,128)S(1)} fusion(bf16[16,256,192]{2,0,1:T(8,128)(2,1)S(1)} %copy.76, bf16[3,256,192]{2,0,1:T(4,128)(2,1)S(1)} %copy-done.4, bf16[3,256,192]{2,0,1:T(4,128)(2,1)S(1)} %copy.75, bf16[22,259,192]{2,0,1:T(8,128)(2,1)S(1)} %get-tuple-element.394, bf16[22,259,192]{2,0,1:T(8,128)(2,1)S(1)} %get-tuple-element.393, ...), kind=kLoop, calls=%fused_computation.143 | loop fusion | flops 129761280 | bytes 71407104 | tf_op jit(solution)/shard_map/add | solution.py:91
  85.1 4.4 %copy.93 = f32[16,256,192]{2,1,0:T(8,128)} copy(f32[16,256,192]{2,0,1:T(8,128)S(1)} %add_add_fusion) | data formatting | bytes 6291456 | tf_op jit(solution)/shard_map/while | solution.py:110
  89.6 61.2 %while.53 = (s32[]{:T(128)}, bf16[8,512,192]{1,2,0:T(8,128)(2,1)S(1)}, bf16[8,512,192]{1,2,0:T(8,128)(2,1)}, f32[192]{0:T(256)S(1)}, f32[8,512,192]{2,1,0:T(8,12...) while((s32[]{:T(128)}, ...), condition=%wide.region_3.4_spmd, body=%wide.region_0.3_spmd.sunk | while | flops 329318912 | bytes 2321533 | solution.py:110
  92.2 5.1 %fusion.140 = bf16[8,512,192]{1,2,0:T(8,128)(2,1)S(1)} fusion(bf16[8,512,192]{1,2,0:T(8,128)(2,1)S(1)} %get-tuple-element.703, s32[]{:T(128)} %get-tuple-element.702, bf16[768,192]{0,1:T(8,128)(2,1)S(1)} %get-tuple-element.723, bf16[192,768]{1,0:T(8,128)(2,1)S(1)} %get-tuple-element.721, f32[768]{0:T(1024)S(1)} %get-tuple-element.722, ...), kind=kOutput, calls=%fused_computation.25.clone.1 | convolution fusion | flops 328925184 | bytes 1520640 | tf_op jit(solution)/shard_map/while/body/eval_jaxpr/dot_general | solution.py:107
  99.9 5.1 %fusion.140 = bf16[8,512,192]{1,2,0:T(8,128)(2,1)S(1)} fusion(bf16[8,512,192]{1,2,0:T(8,128)(2,1)S(1)} %get-tuple-element.703, s32[]{:T(128)} %get-tuple-element.702, bf16[768,192]{0,1:T(8,128)(2,1)S(1)} %get-tuple-element.723, bf16[192,768]{1,0:T(8,128)(2,1)S(1)} %get-tuple-element.721, f32[768]{0:T(1024)S(1)} %get-tuple-element.722, ...), kind=kOutput, calls=%fused_computation.25.clone.1 | convolution fusion | flops 328925184 | bytes 1520640 | tf_op jit(solution)/shard_map/while/body/eval_jaxpr/dot_general | solution.py:107
  107.5 5.1 %fusion.140 = bf16[8,512,192]{1,2,0:T(8,128)(2,1)S(1)} fusion(bf16[8,512,192]{1,2,0:T(8,128)(2,1)S(1)} %get-tuple-element.703, s32[]{:T(128)} %get-tuple-element.702, bf16[768,192]{0,1:T(8,128)(2,1)S(1)} %get-tuple-element.723, bf16[192,768]{1,0:T(8,128)(2,1)S(1)} %get-tuple-element.721, f32[768]{0:T(1024)S(1)} %get-tuple-element.722, ...), kind=kOutput, calls=%fused_computation.25.clone.1 | convolution fusion | flops 328925184 | bytes 1520640 | tf_op jit(solution)/shard_map/while/body/eval_jaxpr/dot_general | solution.py:107
  115.1 5.1 %fusion.140 = bf16[8,512,192]{1,2,0:T(8,128)(2,1)S(1)} fusion(bf16[8,512,192]{1,2,0:T(8,128)(2,1)S(1)} %get-tuple-element.703, s32[]{:T(128)} %get-tuple-element.702, bf16[768,192]{0,1:T(8,128)(2,1)S(1)} %get-tuple-element.723, bf16[192,768]{1,0:T(8,128)(2,1)S(1)} %get-tuple-element.721, f32[768]{0:T(1024)S(1)} %get-tuple-element.722, ...), kind=kOutput, calls=%fused_computation.25.clone.1 | convolution fusion | flops 328925184 | bytes 1520640 | tf_op jit(solution)/shard_map/while/body/eval_jaxpr/dot_general | solution.py:107
  122.8 5.1 %fusion.140 = bf16[8,512,192]{1,2,0:T(8,128)(2,1)S(1)} fusion(bf16[8,512,192]{1,2,0:T(8,128)(2,1)S(1)} %get-tuple-element.703, s32[]{:T(128)} %get-tuple-element.702, bf16[768,192]{0,1:T(8,128)(2,1)S(1)} %get-tuple-element.723, bf16[192,768]{1,0:T(8,128)(2,1)S(1)} %get-tuple-element.721, f32[768]{0:T(1024)S(1)} %get-tuple-element.722, ...), kind=kOutput, calls=%fused_computation.25.clone.1 | convolution fusion | flops 328925184 | bytes 1520640 | tf_op jit(solution)/shard_map/while/body/eval_jaxpr/dot_general | solution.py:107
  130.4 5.1 %fusion.140 = bf16[8,512,192]{1,2,0:T(8,128)(2,1)S(1)} fusion(bf16[8,512,192]{1,2,0:T(8,128)(2,1)S(1)} %get-tuple-element.703, s32[]{:T(128)} %get-tuple-element.702, bf16[768,192]{0,1:T(8,128)(2,1)S(1)} %get-tuple-element.723, bf16[192,768]{1,0:T(8,128)(2,1)S(1)} %get-tuple-element.721, f32[768]{0:T(1024)S(1)} %get-tuple-element.722, ...), kind=kOutput, calls=%fused_computation.25.clone.1 | convolution fusion | flops 328925184 | bytes 1520640 | tf_op jit(solution)/shard_map/while/body/eval_jaxpr/dot_general | solution.py:107
  138.0 5.1 %fusion.140 = bf16[8,512,192]{1,2,0:T(8,128)(2,1)S(1)} fusion(bf16[8,512,192]{1,2,0:T(8,128)(2,1)S(1)} %get-tuple-element.703, s32[]{:T(128)} %get-tuple-element.702, bf16[768,192]{0,1:T(8,128)(2,1)S(1)} %get-tuple-element.723, bf16[192,768]{1,0:T(8,128)(2,1)S(1)} %get-tuple-element.721, f32[768]{0:T(1024)S(1)} %get-tuple-element.722, ...), kind=kOutput, calls=%fused_computation.25.clone.1 | convolution fusion | flops 328925184 | bytes 1520640 | tf_op jit(solution)/shard_map/while/body/eval_jaxpr/dot_general | solution.py:107
  145.7 5.1 %fusion.140 = bf16[8,512,192]{1,2,0:T(8,128)(2,1)S(1)} fusion(bf16[8,512,192]{1,2,0:T(8,128)(2,1)S(1)} %get-tuple-element.703, s32[]{:T(128)} %get-tuple-element.702, bf16[768,192]{0,1:T(8,128)(2,1)S(1)} %get-tuple-element.723, bf16[192,768]{1,0:T(8,128)(2,1)S(1)} %get-tuple-element.721, f32[768]{0:T(1024)S(1)} %get-tuple-element.722, ...), kind=kOutput, calls=%fused_computation.25.clone.1 | convolution fusion | flops 328925184 | bytes 1520640 | tf_op jit(solution)/shard_map/while/body/eval_jaxpr/dot_general | solution.py:107
  152.5 1.9 copy_bitcast_fusion
  154.4 86.8 %while.56 = (s32[]{:T(128)}, f32[8,512]{1,0:T(8,128)S(1)}, f32[8,512]{1,0:T(8,128)S(1)}, f32[8,512,24]{1,2,0:T(8,128)S(1)}, s32[8,512]{1,0:T(8,128)S(1)}, /*inde...) while((s32[]{:T(128)}, f32[8,512]{1,0:T(8,128)S(1)}, ...), condition=%wide.region_10.11_spmd.clone, body=%wide.region_4.10_spmd.clone.sunk | while | flops 225448448 | bytes 29871736 | solution.py:136
  155.5 2.3 bitcast_reduce_fusion.3
  157.9 4.1 %convert_reduce_fusion.2 = (f32[4,8,512]{2,0,1:T(4,128)S(1)}, bf16[4,8,512,128]{2,3,0,1:T(8,128)(2,1)}) fusion(f32[4,8,512]{2,0,1:T(4,128)S(1)} %is-finite_select_fusion.2, f32[8,4,128,512]{3,2,1,0:T(8,128)S(1)} %get-tuple-element.682, pred[4,128]{1,0:T(4,128)(4,1)S(1)} %bitcast.188), kind=kLoop, calls=%fused_computation.120.clone.1 | loop fusion | flops 14663680 | bytes 12714496 | tf_op jit(solution)/shard_map/while/body/eval_jaxpr/reduce_sum | solution.py:44
  162.1 2.9 multiply_reduce_fusion.8
  166.4 2.3 bitcast_reduce_fusion.3
  168.7 4.1 %convert_reduce_fusion.2 = (f32[4,8,512]{2,0,1:T(4,128)S(1)}, bf16[4,8,512,128]{2,3,0,1:T(8,128)(2,1)}) fusion(f32[4,8,512]{2,0,1:T(4,128)S(1)} %is-finite_select_fusion.2, f32[8,4,128,512]{3,2,1,0:T(8,128)S(1)} %get-tuple-element.682, pred[4,128]{1,0:T(4,128)(4,1)S(1)} %bitcast.188), kind=kLoop, calls=%fused_computation.120.clone.1 | loop fusion | flops 14663680 | bytes 12714496 | tf_op jit(solution)/shard_map/while/body/eval_jaxpr/reduce_sum | solution.py:44
  173.0 2.9 multiply_reduce_fusion.8
  177.2 2.3 bitcast_reduce_fusion.3
  179.6 4.1 %convert_reduce_fusion.2 = (f32[4,8,512]{2,0,1:T(4,128)S(1)}, bf16[4,8,512,128]{2,3,0,1:T(8,128)(2,1)}) fusion(f32[4,8,512]{2,0,1:T(4,128)S(1)} %is-finite_select_fusion.2, f32[8,4,128,512]{3,2,1,0:T(8,128)S(1)} %get-tuple-element.682, pred[4,128]{1,0:T(4,128)(4,1)S(1)} %bitcast.188), kind=kLoop, calls=%fused_computation.120.clone.1 | loop fusion | flops 14663680 | bytes 12714496 | tf_op jit(solution)/shard_map/while/body/eval_jaxpr/reduce_sum | solution.py:44
  183.9 2.9 multiply_reduce_fusion.8
  188.1 2.3 bitcast_reduce_fusion.3
  190.4 4.1 %convert_reduce_fusion.2 = (f32[4,8,512]{2,0,1:T(4,128)S(1)}, bf16[4,8,512,128]{2,3,0,1:T(8,128)(2,1)}) fusion(f32[4,8,512]{2,0,1:T(4,128)S(1)} %is-finite_select_fusion.2, f32[8,4,128,512]{3,2,1,0:T(8,128)S(1)} %get-tuple-element.682, pred[4,128]{1,0:T(4,128)(4,1)S(1)} %bitcast.188), kind=kLoop, calls=%fused_computation.120.clone.1 | loop fusion | flops 14663680 | bytes 12714496 | tf_op jit(solution)/shard_map/while/body/eval_jaxpr/reduce_sum | solution.py:44
  194.7 2.9 multiply_reduce_fusion.8
  198.9 2.3 bitcast_reduce_fusion.3
  201.3 4.1 %convert_reduce_fusion.2 = (f32[4,8,512]{2,0,1:T(4,128)S(1)}, bf16[4,8,512,128]{2,3,0,1:T(8,128)(2,1)}) fusion(f32[4,8,512]{2,0,1:T(4,128)S(1)} %is-finite_select_fusion.2, f32[8,4,128,512]{3,2,1,0:T(8,128)S(1)} %get-tuple-element.682, pred[4,128]{1,0:T(4,128)(4,1)S(1)} %bitcast.188), kind=kLoop, calls=%fused_computation.120.clone.1 | loop fusion | flops 14663680 | bytes 12714496 | tf_op jit(solution)/shard_map/while/body/eval_jaxpr/reduce_sum | solution.py:44
  205.5 2.9 multiply_reduce_fusion.8
  209.8 2.3 bitcast_reduce_fusion.3
  212.1 4.1 %convert_reduce_fusion.2 = (f32[4,8,512]{2,0,1:T(4,128)S(1)}, bf16[4,8,512,128]{2,3,0,1:T(8,128)(2,1)}) fusion(f32[4,8,512]{2,0,1:T(4,128)S(1)} %is-finite_select_fusion.2, f32[8,4,128,512]{3,2,1,0:T(8,128)S(1)} %get-tuple-element.682, pred[4,128]{1,0:T(4,128)(4,1)S(1)} %bitcast.188), kind=kLoop, calls=%fused_computation.120.clone.1 | loop fusion | flops 14663680 | bytes 12714496 | tf_op jit(solution)/shard_map/while/body/eval_jaxpr/reduce_sum | solution.py:44
  216.4 2.9 multiply_reduce_fusion.8
  220.7 2.3 bitcast_reduce_fusion.3
  223.0 4.1 %convert_reduce_fusion.2 = (f32[4,8,512]{2,0,1:T(4,128)S(1)}, bf16[4,8,512,128]{2,3,0,1:T(8,128)(2,1)}) fusion(f32[4,8,512]{2,0,1:T(4,128)S(1)} %is-finite_select_fusion.2, f32[8,4,128,512]{3,2,1,0:T(8,128)S(1)} %get-tuple-element.682, pred[4,128]{1,0:T(4,128)(4,1)S(1)} %bitcast.188), kind=kLoop, calls=%fused_computation.120.clone.1 | loop fusion | flops 14663680 | bytes 12714496 | tf_op jit(solution)/shard_map/while/body/eval_jaxpr/reduce_sum | solution.py:44
  227.3 2.9 multiply_reduce_fusion.8
  231.5 2.3 bitcast_reduce_fusion.3
  233.8 4.1 %convert_reduce_fusion.2 = (f32[4,8,512]{2,0,1:T(4,128)S(1)}, bf16[4,8,512,128]{2,3,0,1:T(8,128)(2,1)}) fusion(f32[4,8,512]{2,0,1:T(4,128)S(1)} %is-finite_select_fusion.2, f32[8,4,128,512]{3,2,1,0:T(8,128)S(1)} %get-tuple-element.682, pred[4,128]{1,0:T(4,128)(4,1)S(1)} %bitcast.188), kind=kLoop, calls=%fused_computation.120.clone.1 | loop fusion | flops 14663680 | bytes 12714496 | tf_op jit(solution)/shard_map/while/body/eval_jaxpr/reduce_sum | solution.py:44
  238.1 2.9 multiply_reduce_fusion.8
  242.0 5.2 %all-gather = f32[32,512]{1,0:T(8,128)S(1)} all-gather(f32[8,512]{1,0:T(8,128)S(1)} %get-tuple-element.181), channel_id=2, replica_groups=mesh['row'=8,'col'=4] {'col'}, dimensions={0}, use_global_device_ids=true | all-gather | bytes 81920 | tf_op jit(solution)/shard_map/all_gather | solution.py:23
  247.2 5.6 %all-gather.1 = f32[32,512]{1,0:T(8,128)S(1)} all-gather(f32[8,512]{1,0:T(8,128)S(1)} %get-tuple-element.182), channel_id=3, replica_groups=mesh['row'=8,'col'=4] {'col'}, dimensions={0}, use_global_device_ids=true | all-gather | bytes 81920 | tf_op jit(solution)/shard_map/all_gather | solution.py:23
  252.8 11.2 %all-gather.9.cloned.1.call-done = f32[32,512,24]{1,2,0:T(8,128)} async-done(((f32[8,512,24]{1,2,0:T(8,128)}), f32[32,512,24]{1,2,0:T(8,128)}) %all-gather.9.cloned.1.call-update) | async-done | bytes 1572880 | tf_op jit(solution)/shard_map/all_gather | solution.py:23
  269.6 1.7 copy.90
  271.3 24.6 %all-gather.3 = f32[64,512]{1,0:T(8,128)S(1)} all-gather(f32[8,512]{1,0:T(8,128)S(1)} %get-tuple-element.184), channel_id=5, replica_groups=mesh['row'=8,'col'=4] {'row'}, dimensions={0}, use_global_device_ids=true | all-gather | bytes 147456 | tf_op jit(solution)/shard_map/all_gather | solution.py:23
  295.9 25.5 %all-gather.4 = f32[64,512]{1,0:T(8,128)S(1)} all-gather(f32[8,512]{1,0:T(8,128)S(1)} %get-tuple-element.185), channel_id=6, replica_groups=mesh['row'=8,'col'=4] {'row'}, dimensions={0}, use_global_device_ids=true | all-gather | bytes 147456 | tf_op jit(solution)/shard_map/all_gather | solution.py:23
  321.4 8.7 %all-gather.11.cloned.1.call-done = f32[64,512,24]{1,2,0:T(8,128)} async-done(((f32[8,512,24]{1,2,0:T(8,128)}), f32[64,512,24]{1,2,0:T(8,128)}) %all-gather.11.cloned.1.call-update) | async-done | bytes 3145744 | tf_op jit(solution)/shard_map/all_gather | solution.py:23
  330.1 2.0 slice.573
  332.1 1.8 slice.570
  333.9 13.0 %while.55 = (s32[]{:T(128)}, f32[8,512]{1,0:T(8,128)S(1)}, f32[8,512]{1,0:T(8,128)S(1)}, f32[8,512,24]{1,2,0:T(8,128)}, f32[7,8,512]{2,1,0:T(8,128)S(1)}, /*inde...) while((s32[]{:T(128)}, f32[8,512]{1,0:T(8,128)S(1)}, f32[8,512]{1,0:T(8,128)S(1)}, ...), condition=%wide.region_14.15_spmd, body=%wide.region_13.14_spmd.sunk | while | flops 319490 | bytes 1343581 | solution.py:26
  334.0 1.8 fusion.144
  335.8 1.8 fusion.144
  337.7 1.8 fusion.144
  339.5 1.8 fusion.144
  341.4 1.8 fusion.144
  343.2 1.8 fusion.144
  345.1 1.8 fusion.144
  (250 shorter events, 48.4 us)
Async XLA Ops:
  7.2 143.8 %copy-start = (bf16[192,192]{1,0:T(8,128)(2,1)S(1)}, bf16[192,192]{1,0:T(8,128)(2,1)}, u32[]{:S(2)}) copy-start(bf16[192,192]{1,0:T(8,128)(2,1)} %param.34) | copy-start | bytes 221188
  7.2 11.5 %copy-start.10 = (f32[7,7,192]{2,1,0:T(8,128)S(1)}, f32[7,7,192]{2,1,0:T(8,128)}, u32[]{:S(2)}) copy-start(f32[7,7,192]{2,1,0:T(8,128)} %param.25) | copy-start | bytes 112900
  7.2 256.8 %all-gather.9.cloned.1.call-start = ((), (), s32[]{:S(2)}) async-start(), calls=%async_computation | async-start | bytes 1966080 | tf_op jit(solution)/shard_map/all_gather | solution.py:23
  9.1 15.9 %collective-permute-start = (bf16[3,256,192]{1,2,0:T(8,128)(2,1)S(1)}, bf16[3,256,192]{1,2,0:T(8,128)(2,1)S(1)}, u32[]{:S(2)}, u32[]{:S(2)}) collective-permute-start(bf16[3,256,192]{1,2,0:T(8,128)(2,1)S(1)} %get-tuple-element.397), channel_id=1, source_target_pairs={{0,4},{4,8},{8,12},{12,16},{16,20},{20,24},{24,28},{1,5},{5,9},{9,... | collective-permute-start | bytes 884744 | tf_op jit(solution)/shard_map/ppermute | solution.py:16
  13.1 12.3 %collective-permute-start.1 = (bf16[3,256,192]{1,2,0:T(8,128)(2,1)}, bf16[3,256,192]{1,2,0:T(8,128)(2,1)S(1)}, u32[]{:S(2)}, u32[]{:S(2)}) collective-permute-start(bf16[3,256,192]{1,2,0:T(8,128)(2,1)} %get-tuple-element.398), channel_id=1, source_target_pairs={{4,0},{8,4},{12,8},{16,12},{20,16},{24,20},{28,24},{5,1},{9,5},{13... | collective-permute-start | bytes 884744 | tf_op jit(solution)/shard_map/ppermute | solution.py:17
  26.4 8.0 %copy-start.3 = (bf16[16,256,192]{1,2,0:T(8,128)(2,1)S(1)}, bf16[16,256,192]{1,2,0:T(8,128)(2,1)}, u32[]{:S(2)}) copy-start(bf16[16,256,192]{1,2,0:T(8,128)(2,1)} %param.23) | copy-start | bytes 4718596
  27.2 16.0 %collective-permute-start.2 = (bf16[22,3,192]{2,0,1:T(8,128)(2,1)S(1)}, bf16[22,3,192]{2,0,1:T(8,128)(2,1)S(1)}, u32[]{:S(2)}, u32[]{:S(2)}) collective-permute-start(bf16[22,3,192]{2,0,1:T(8,128)(2,1)S(1)} %get-tuple-element.395), channel_id=1, source_target_pairs={{0,1},{1,2},{2,3},{4,5},{5,6},{6,7},{8,9},{9,10},{10,11},{12,13},{... | collective-permute-start | bytes 76040 | tf_op jit(solution)/shard_map/ppermute | solution.py:16
  31.8 11.5 %collective-permute-start.3 = (bf16[22,3,192]{2,0,1:T(8,128)(2,1)S(1)}, bf16[22,3,192]{2,0,1:T(8,128)(2,1)S(1)}, u32[]{:S(2)}, u32[]{:S(2)}) collective-permute-start(bf16[22,3,192]{2,0,1:T(8,128)(2,1)S(1)} %get-tuple-element.396), channel_id=1, source_target_pairs={{1,0},{2,1},{3,2},{5,4},{6,5},{7,6},{9,8},{10,9},{11,10},{13,12},{... | collective-permute-start | bytes 76040 | tf_op jit(solution)/shard_map/ppermute | solution.py:17
  34.3 8.7 %copy-start.11 = (s32[16,256]{1,0:T(8,128)S(1)}, s32[16,256]{1,0:T(8,128)}, u32[]{:S(2)}) copy-start(s32[16,256]{1,0:T(8,128)} %param.24) | copy-start | bytes 49156
  43.1 7.7 %copy-start.4 = (bf16[3,256,192]{2,0,1:T(4,128)(2,1)S(1)}, bf16[3,256,192]{2,0,1:T(4,128)(2,1)}, u32[]{:S(2)}) copy-start(bf16[3,256,192]{2,0,1:T(4,128)(2,1)} %copy.77) | copy-start | bytes 884740
  43.1 7.7 %copy-start.12 = (f32[1,1,192]{2,1,0:T(1,128)S(1)}, f32[1,1,192]{2,1,0:T(1,128)}, u32[]{:S(2)}) copy-start(f32[1,1,192]{2,1,0:T(1,128)} %get-tuple-element.402) | copy-start | bytes 2308
  43.1 7.7 %copy-start.13 = (f32[1,1,192]{2,1,0:T(1,128)S(1)}, f32[1,1,192]{2,1,0:T(1,128)}, u32[]{:S(2)}) copy-start(f32[1,1,192]{2,1,0:T(1,128)} %get-tuple-element.403) | copy-start | bytes 2308
  43.1 7.7 %copy-start.14 = (f32[1,1,192]{2,1,0:T(1,128)S(1)}, f32[1,1,192]{2,1,0:T(1,128)}, u32[]{:S(2)}) copy-start(f32[1,1,192]{2,1,0:T(1,128)} %get-tuple-element.404) | copy-start | bytes 2308
  43.1 7.7 %copy-start.15 = (f32[1,1,192]{2,1,0:T(1,128)S(1)}, f32[1,1,192]{2,1,0:T(1,128)}, u32[]{:S(2)}) copy-start(f32[1,1,192]{2,1,0:T(1,128)} %get-tuple-element.405) | copy-start | bytes 2308
  43.1 7.7 %copy-start.16 = (f32[1,1,192]{2,1,0:T(1,128)S(1)}, f32[1,1,192]{2,1,0:T(1,128)}, u32[]{:S(2)}) copy-start(f32[1,1,192]{2,1,0:T(1,128)} %get-tuple-element.406) | copy-start | bytes 2308
  43.1 7.7 %copy-start.17 = (f32[1,1,192]{2,1,0:T(1,128)S(1)}, f32[1,1,192]{2,1,0:T(1,128)}, u32[]{:S(2)}) copy-start(f32[1,1,192]{2,1,0:T(1,128)} %get-tuple-element.407) | copy-start | bytes 2308
  43.1 7.7 %copy-start.18 = (f32[1,1,192]{2,1,0:T(1,128)S(1)}, f32[1,1,192]{2,1,0:T(1,128)}, u32[]{:S(2)}) copy-start(f32[1,1,192]{2,1,0:T(1,128)} %get-tuple-element.408) | copy-start | bytes 2308
  43.2 7.7 %copy-start.19 = (f32[1,1,192]{2,1,0:T(1,128)S(1)}, f32[1,1,192]{2,1,0:T(1,128)}, u32[]{:S(2)}) copy-start(f32[1,1,192]{2,1,0:T(1,128)} %get-tuple-element.409) | copy-start | bytes 2308
  43.2 7.7 %copy-start.20 = (f32[1,1,192]{2,1,0:T(1,128)S(1)}, f32[1,1,192]{2,1,0:T(1,128)}, u32[]{:S(2)}) copy-start(f32[1,1,192]{2,1,0:T(1,128)} %get-tuple-element.410) | copy-start | bytes 2308
  43.2 7.7 %copy-start.21 = (f32[1,1,192]{2,1,0:T(1,128)S(1)}, f32[1,1,192]{2,1,0:T(1,128)}, u32[]{:S(2)}) copy-start(f32[1,1,192]{2,1,0:T(1,128)} %get-tuple-element.411) | copy-start | bytes 2308
  43.2 7.7 %copy-start.22 = (f32[1,1,192]{2,1,0:T(1,128)S(1)}, f32[1,1,192]{2,1,0:T(1,128)}, u32[]{:S(2)}) copy-start(f32[1,1,192]{2,1,0:T(1,128)} %get-tuple-element.412) | copy-start | bytes 2308
  43.2 7.7 %copy-start.23 = (f32[1,1,192]{2,1,0:T(1,128)S(1)}, f32[1,1,192]{2,1,0:T(1,128)}, u32[]{:S(2)}) copy-start(f32[1,1,192]{2,1,0:T(1,128)} %get-tuple-element.413) | copy-start | bytes 2308
  43.2 7.7 %copy-start.24 = (f32[1,1,192]{2,1,0:T(1,128)S(1)}, f32[1,1,192]{2,1,0:T(1,128)}, u32[]{:S(2)}) copy-start(f32[1,1,192]{2,1,0:T(1,128)} %get-tuple-element.414) | copy-start | bytes 2308
  43.2 7.7 %copy-start.25 = (f32[1,1,192]{2,1,0:T(1,128)S(1)}, f32[1,1,192]{2,1,0:T(1,128)}, u32[]{:S(2)}) copy-start(f32[1,1,192]{2,1,0:T(1,128)} %get-tuple-element.415) | copy-start | bytes 2308
  43.2 7.7 %copy-start.26 = (f32[1,1,192]{2,1,0:T(1,128)S(1)}, f32[1,1,192]{2,1,0:T(1,128)}, u32[]{:S(2)}) copy-start(f32[1,1,192]{2,1,0:T(1,128)} %get-tuple-element.416) | copy-start | bytes 2308
  43.2 7.7 %copy-start.27 = (f32[1,1,192]{2,1,0:T(1,128)S(1)}, f32[1,1,192]{2,1,0:T(1,128)}, u32[]{:S(2)}) copy-start(f32[1,1,192]{2,1,0:T(1,128)} %get-tuple-element.417) | copy-start | bytes 2308
  43.2 7.7 %copy-start.28 = (f32[1,1,192]{2,1,0:T(1,128)S(1)}, f32[1,1,192]{2,1,0:T(1,128)}, u32[]{:S(2)}) copy-start(f32[1,1,192]{2,1,0:T(1,128)} %get-tuple-element.445) | copy-start | bytes 2308
  43.3 7.7 %copy-start.29 = (f32[1,1,192]{2,1,0:T(1,128)S(1)}, f32[1,1,192]{2,1,0:T(1,128)}, u32[]{:S(2)}) copy-start(f32[1,1,192]{2,1,0:T(1,128)} %get-tuple-element.446) | copy-start | bytes 2308
  43.3 7.7 %copy-start.30 = (f32[1,1,192]{2,1,0:T(1,128)S(1)}, f32[1,1,192]{2,1,0:T(1,128)}, u32[]{:S(2)}) copy-start(f32[1,1,192]{2,1,0:T(1,128)} %get-tuple-element.447) | copy-start | bytes 2308
  43.3 7.7 %copy-start.31 = (f32[192]{0:T(256)S(1)}, f32[192]{0:T(256)}, u32[]{:S(2)}) copy-start(f32[192]{0:T(256)} %param.26) | copy-start | bytes 2308
  85.0 4.5 %copy-start.5 = (bf16[8,512,192]{1,2,0:T(8,128)(2,1)S(1)}, bf16[8,512,192]{1,2,0:T(8,128)(2,1)}, u32[]{:S(2)}) copy-start(bf16[8,512,192]{1,2,0:T(8,128)(2,1)} %custom-call.3) | copy-start | bytes 4718596
  85.0 4.5 %copy-start.32 = (bf16[192,768]{1,0:T(8,128)(2,1)S(1)}, bf16[192,768]{1,0:T(8,128)(2,1)}, u32[]{:S(2)}) copy-start(bf16[192,768]{1,0:T(8,128)(2,1)} %param.29) | copy-start | bytes 884740
  85.0 4.5 %copy-start.33 = (bf16[768,192]{0,1:T(8,128)(2,1)S(1)}, bf16[768,192]{0,1:T(8,128)(2,1)}, u32[]{:S(2)}) copy-start(bf16[768,192]{0,1:T(8,128)(2,1)} %param.31) | copy-start | bytes 884740
  85.0 4.5 %copy-start.35 = (f32[768]{0:T(1024)S(1)}, f32[768]{0:T(1024)}, u32[]{:S(2)}) copy-start(f32[768]{0:T(1024)} %param.30) | copy-start | bytes 9220
  85.1 4.5 %copy-start.36 = (f32[192]{0:T(256)S(1)}, f32[192]{0:T(256)}, u32[]{:S(2)}) copy-start(f32[192]{0:T(256)} %param.33) | copy-start | bytes 2308
  85.1 4.5 %copy-start.37 = (f32[192]{0:T(256)S(1)}, f32[192]{0:T(256)}, u32[]{:S(2)}) copy-start(f32[192]{0:T(256)} %param.27) | copy-start | bytes 2308
  85.1 4.5 %copy-start.38 = (f32[192]{0:T(256)S(1)}, f32[192]{0:T(256)}, u32[]{:S(2)}) copy-start(f32[192]{0:T(256)} %param.28) | copy-start | bytes 2308
  85.1 4.5 %copy-start.39 = (f32[192]{0:T(256)S(1)}, f32[192]{0:T(256)}, u32[]{:S(2)}) copy-start(f32[192]{0:T(256)} %param.32) | copy-start | bytes 2308
  150.8 1.6 copy-start.6
  150.8 1.0 copy-start.8
  151.8 2.6 copy-start.34
  241.2 0.7 copy-start.2
  242.0 88.1 %all-gather.11.cloned.1.call-start = ((), (), s32[]{:S(2)}) async-start(), calls=%async_computation.1 | async-start | bytes 3538944 | tf_op jit(solution)/shard_map/all_gather | solution.py:23
  265.4 2.8 copy-start.7
  267.4 0.7 copy-start.1
  332.1 15.8 %copy-start.9 = (bf16[192,192]{1,0:T(8,128)(2,1)S(1)}, bf16[192,192]{1,0:T(8,128)(2,1)}, u32[]{:S(2)}) copy-start(bf16[192,192]{1,0:T(8,128)(2,1)} %param.37) | copy-start | bytes 221188
Sparse Core Ops, SparseCore 0:
  242.1 21.8 all-gather.8
  268.3 61.7 all-gather.10
where the time goes:
time: 362 us; the launch traced here: 356 us
  other arithmetic  112 us (31%)
  matrix products  84.5 us (23%)
  blocking collectives  60.8 us (17%)
  local copies, waits for them, and re-layouts  44.7 us (12%)
  waiting for transfers between devices  25.6 us (7%)
  between operations  14.8 us (4%)
  starting transfers between devices  11.8 us (3%)
    all_gather x4, blocking collectives, merged_2(): pieces = jax.tree.map(lambda part: lax.all_gather(part, axis), value)  60.8 us
    dot_general x8, matrix products, mlp_block(): branch = jnp.dot(hidden, w_out, preferred_element_type=jnp.float32) + b_out  41 us
    add x1, other arithmetic, body(): conv = conv + dw_bias  34 us
    reduce_sum x8, other arithmetic, pool_group(): tile_total = jnp.sum(weights.astype(jnp.float32), axis=-1)  32.8 us
    dot_general x8, matrix products, pool_group(): jnp.einsum('thqp,tphd->thqd', weights, value_tiles, preferred_element_typ...  23 us
    all_gather x2, waiting for transfers between devices, merged_2(): pieces = jax.tree.map(lambda part: lax.all_gather(part, axis), value)  19.9 us
    dot_general x8, matrix products, pool_group(): jnp.einsum('qhd,tphd->thqp', query_heads, key_tiles, preferred_element_ty...  18.3 us
    add x10, other arithmetic, combine_parts(): accum = first[2] * left[..., None] + second[2] * right[..., None]  13.3 us
  transfers between devices with their start and end apart: 6, of which 3 were waited for; matrix products, arithmetic and copies ran while one was open for 5% of the time, Pallas kernels for 0%

commit v1 on v0

v1 whole, which is shorter than its diff:
```python
import functools
import math

import jax
import jax.numpy as jnp
from jax import lax
from jax.experimental import pallas as pl
from jax.experimental.pallas import tpu as pltpu
from jax.sharding import PartitionSpec as P

NH = 8
PAD = 16
LOW = -1e29
MASKED = -1e30


def block_kernel(
    rows,
    cols,
    channels,
    hidden,
    query_count,
    x_ref,
    bias_ref,
    dw_ref,
    vec_ref,
    win_ref,
    bin_ref,
    wout_ref,
    wkt_ref,
    wv_ref,
    q_ref,
    out_ref,
    part_ref,
    xf_ref,
    conv_ref,
    kt_ref,
    v_ref,
    sa_ref,
    sb_ref,
):
    positions = rows * cols
    head_size = channels // NH
    depth = kt_ref.shape[0]
    wide = 256
    high = channels - 128

    def widen(i, carry):
        line = x_ref[i].astype(jnp.float32)
        xf_ref[0, i] = line[:, 0:128]
        xf_ref[1, i, :, 0:high] = line[:, 128:channels]
        return carry

    lax.fori_loop(0, rows + 6, widen, 0)

    def conv_tile(tile, carry):
        start = pl.multiple_of(tile * 8, 8)
        for half in range(2):
            acc = [None] * rows
            for b in range(7):
                taps = [dw_ref[half, a, b] for a in range(7)]
                for i in range(rows + 6):
                    window = xf_ref[half, i, pl.ds(start + (PAD - 3 + b), 8), :]
                    for a in range(7):
                        r = i - a
                        if 0 <= r < rows:
                            term = window * taps[a]
                            acc[r] = term if acc[r] is None else acc[r] + term
            for r in range(rows):
                conv_ref[r, pl.ds(start, 8), half * 128 : half * 128 + 128] = acc[r]
        return carry

    lax.fori_loop(0, cols // 8, conv_tile, 0)

    block = 2 * cols
    dw_bias = vec_ref[0:1, :]
    gain = vec_ref[1:2, :]
    shift = vec_ref[2:3, :]
    b_out = vec_ref[3:4, :]
    scale = vec_ref[4:5, :]
    kt_ref[channels:depth, :] = jnp.zeros((depth - channels, positions), jnp.bfloat16)
    kt_ref[channels : channels + 16, :] = bias_ref[...]
    lane16 = lax.broadcasted_iota(jnp.int32, (positions, wide - channels), 1)
    v_ref[:, channels:wide] = jnp.where(lane16 < NH, 1.0, 0.0).astype(jnp.bfloat16)

    def mlp(step, carry):
        row = step * 2
        flat = conv_ref[pl.ds(row, 2)].reshape(block, wide)[:, 0:channels] + dw_bias
        center = x_ref[pl.ds(row + 3, 2), PAD : PAD + cols, :].reshape(block, channels)
        average = jnp.mean(flat, axis=-1, keepdims=True)
        moved = flat - average
        spread = jnp.mean(moved * moved, axis=-1, keepdims=True)
        normed = (moved * lax.rsqrt(spread + 1e-06) * gain + shift).astype(jnp.bfloat16)
        inner = jnp.dot(normed, win_ref[...], preferred_element_type=jnp.float32) + bin_ref[...]
        act = (0.5 * inner * (1.0 + lax.erf(inner * math.sqrt(0.5)))).astype(jnp.bfloat16)
        branch = jnp.dot(act, wout_ref[...], preferred_element_type=jnp.float32) + b_out
        result = (center.astype(jnp.float32) + scale * branch).astype(jnp.bfloat16)
        out_ref[pl.ds(row, 2)] = result.reshape(2, cols, channels)
        first = pl.multiple_of(step * block, block)
        kt_ref[0:channels, pl.ds(first, block)] = lax.dot_general(
            wkt_ref[...], result, (((1,), (1,)), ((), ())), preferred_element_type=jnp.float32
        ).astype(jnp.bfloat16)
        v_ref[pl.ds(first, block), 0:channels] = jnp.dot(
            result, wv_ref[...], preferred_element_type=jnp.float32
        ).astype(jnp.bfloat16)
        return carry

    lax.fori_loop(0, rows // 2, mlp, 0)

    factor = math.log2(math.e) / math.sqrt(head_size)
    qb = sa_ref.shape[0]
    blocks = query_count // qb
    total = NH * blocks
    lane = lax.broadcasted_iota(jnp.int32, (qb, wide), 1)
    owner = jnp.where(
        lane < channels,
        lane // head_size,
        jnp.where(lane < channels + NH, lane - channels, NH),
    )

    def score(index, s_ref):
        first = pl.multiple_of(index * qb, qb)
        s = jnp.dot(
            q_ref[pl.ds(first, qb), :], kt_ref[...], preferred_element_type=jnp.float32
        )
        s_ref[...] = s
        return jnp.maximum(jnp.max(s, axis=-1, keepdims=True), LOW)

    def absorb(index, s_ref, top):
        e = jnp.exp2((s_ref[...] - top) * factor).astype(jnp.bfloat16)
        o = jnp.dot(e, v_ref[...], preferred_element_type=jnp.float32)
        head = index // blocks
        at = pl.multiple_of((index - head * blocks) * qb, qb)
        held = part_ref[pl.ds(at, qb), :]
        held = jnp.where(owner == head, o, held)
        held = jnp.where(lane == channels + NH + head, top * factor, held)
        part_ref[pl.ds(at, qb), :] = held

    part_ref[...] = jnp.zeros_like(part_ref)
    top_a = score(0, sa_ref)

    def attend(pair, top_a):
        index = pair * 2
        top_b = score(index + 1, sb_ref)
        absorb(index, sa_ref, top_a)
        top_a = score(jnp.minimum(index + 2, total - 1), sa_ref)
        absorb(index + 1, sb_ref, top_b)
        return top_a

    lax.fori_loop(0, total // 2, attend, top_a)


def halo(value, axis, dim, width):
    count, length = (lax.axis_size(axis), value.shape[dim])
    up = [(i, i + 1) for i in range(count - 1)]
    down = [(j, i) for i, j in up]
    last = lax.slice_in_dim(value, length - width, length, axis=dim)
    initial = lax.slice_in_dim(value, 0, width, axis=dim)
    before = lax.ppermute(last, axis, up)
    after = lax.ppermute(initial, axis, down)
    return jnp.concatenate([before, value, after], axis=dim)


def body(
    feature,
    mask,
    dw_weight,
    dw_bias,
    ln_gain,
    ln_bias,
    w_in,
    b_in,
    w_out,
    b_out,
    layer_scale,
    w_key,
    w_value,
    queries,
    w_proj,
):
    rows, cols, channels = feature.shape
    positions = rows * cols
    hidden = w_in.shape[1]
    query_count = queries.shape[0]
    head_size = channels // NH
    depth = channels + 16
    padded = halo(halo(feature, "row", 0, 3), "col", 1, PAD)
    bias = jnp.where(mask > 0, 0.0, MASKED).astype(jnp.bfloat16).reshape(1, positions)
    bias = jnp.pad(bias, ((0, 15), (0, 0)))
    dw = jnp.pad(dw_weight, ((0, 0), (0, 0), (0, 256 - channels)))
    dw = jnp.transpose(dw.reshape(7, 7, 2, 128), (2, 0, 1, 3))
    dw = jnp.broadcast_to(dw[:, :, :, None, :], (2, 7, 7, 8, 128))
    vectors = jnp.stack([dw_bias, ln_gain, ln_bias, b_out, layer_scale] + [b_out] * 3)
    channel_head = jnp.arange(channels) // head_size
    own = channel_head[None, :] == jnp.arange(NH)[:, None]
    spread = jnp.where(own[:, None, :], queries[None], 0).astype(jnp.bfloat16)
    tail = jnp.where(jnp.arange(depth - channels) == 0, 1.0, 0.0).astype(jnp.bfloat16)
    tail = jnp.broadcast_to(tail, (NH, query_count, depth - channels))
    q_wide = jnp.concatenate([spread, tail], axis=-1).reshape(NH * query_count, depth)
    qb = 256
    whole = pl.BlockSpec(memory_space=pltpu.VMEM)
    block_out, part = pl.pallas_call(
        functools.partial(block_kernel, rows, cols, channels, hidden, query_count),
        out_shape=(
            jax.ShapeDtypeStruct(feature.shape, jnp.bfloat16),
            jax.ShapeDtypeStruct((query_count, 256), jnp.float32),
        ),
        in_specs=[whole] * 10,
        out_specs=(whole, whole),
        scratch_shapes=[
            pltpu.VMEM((2, rows + 6, cols + 2 * PAD, 128), jnp.float32),
            pltpu.VMEM((rows, cols, 256), jnp.float32),
            pltpu.VMEM((depth, positions), jnp.bfloat16),
            pltpu.VMEM((positions, 256), jnp.bfloat16),
            pltpu.VMEM((qb, positions), jnp.float32),
            pltpu.VMEM((qb, positions), jnp.float32),
        ],
        compiler_params=pltpu.CompilerParams(vmem_limit_bytes=56 << 20),
        name="block",
    )(
        padded,
        bias,
        dw,
        vectors,
        w_in,
        b_in.reshape(1, hidden),
        w_out,
        jnp.transpose(w_key),
        w_value,
        q_wide,
    )
    top = part[:, channels + NH : channels + 2 * NH]
    best = lax.pmax(top, ("row", "col"))
    keep = jnp.exp2(top - best)
    scaled = jnp.concatenate(
        [
            part[:, :channels] * jnp.repeat(keep, head_size, axis=1),
            part[:, channels : channels + NH] * keep,
        ],
        axis=1,
    )
    merged = lax.psum(scaled, ("row", "col"))
    pooled = merged[:, :channels] / jnp.repeat(merged[:, channels:], head_size, axis=1)
    pooled_out = jnp.dot(
        pooled.astype(jnp.bfloat16), w_proj, preferred_element_type=jnp.float32
    )
    return (block_out, pooled_out)


def solution(mesh):
    return jax.shard_map(
        body,
        mesh=mesh,
        in_specs=(P("row", "col", None), P("row", "col")) + (P(),) * 13,
        out_specs=(P("row", "col", None), P()),
        check_vma=False,
    )
```

time: 362 us -> 296 us (0.82); the launches traced: 356 us -> 294 us
  waiting for transfers between devices: 25.6 us -> 138 us
  other arithmetic: 112 us -> 8.04 us
  matrix products: 84.5 us -> 2.05 us
  Pallas kernels: 0 us -> 59.8 us
  local copies, waits for them, and re-layouts: 44.7 us -> 16.9 us
  blocking collectives: 60.8 us -> 43.1 us
    psum x0 -> x1, waiting for transfers between devices: none -> 126 us  [body(): merged = lax.psum(scaled, ('row', 'col'))]
    dot_general x27 -> x1, matrix products: 84.5 us -> 2.05 us  [body(): jnp.dot(pooled.astype(jnp.bfloat16), w_proj, preferred_element_type=jnp.f...]
    all_gather x4 -> x0, blocking collectives: 60.8 us -> none  [merged_2(): pieces = jax.tree.map(lambda part: lax.all_gather(part, axis), value)]
    pallas_call x0 -> x1, Pallas kernels: none -> 59.8 us  [body(): pl.pallas_call(functools.partial(block_kernel, rows, cols, channels, hidd...]
    reduce_sum x32 -> x0, other arithmetic: 53.1 us -> none  [the longest x8 32.8 us: pool_group(): tile_total = jnp.sum(weights.astype(jnp.float32), axis=-1)]
    add x37 -> x0, other arithmetic: 49 us -> none  [the longest x1 34 us: body(): conv = conv + dw_bias]
    pmax x0 -> x1, blocking collectives: none -> 43.1 us  [body(): best = lax.pmax(top, ('row', 'col'))]
    all_gather x2 -> x0, waiting for transfers between devices: 19.9 us -> none  [merged_2(): pieces = jax.tree.map(lambda part: lax.all_gather(part, axis), value)]
  transfers between devices with their start and end apart: 6 -> 5, of which waited for: 3 -> 3; matrix products, arithmetic and copies ran while one was open for 5% -> 4% of each run, Pallas kernels for 0% -> 0%
where the time goes in v1:
time: 296 us; the launch traced here: 294 us
  waiting for transfers between devices  138 us (47%)
  Pallas kernels  59.8 us (20%)
  blocking collectives  43.1 us (15%)
  local copies, waits for them, and re-layouts  16.9 us (6%)
  between operations  14.3 us (5%)
  starting transfers between devices  11.8 us (4%)
  other arithmetic  8.04 us (3%)
    psum x1, waiting for transfers between devices, body(): merged = lax.psum(scaled, ('row', 'col'))  126 us
    pallas_call x1, Pallas kernels, body(): pl.pallas_call(functools.partial(block_kernel, rows, cols, channels, hidd...  59.8 us
    pmax x1, blocking collectives, body(): best = lax.pmax(top, ('row', 'col'))  43.1 us
    ppermute x2, waiting for transfers between devices, halo(): before = lax.ppermute(last, axis, up)  11.7 us
    ppermute x2, starting transfers between devices, halo(): before = lax.ppermute(last, axis, up)  8.52 us
    unnamed x26, local copies, waits for them, and re-layouts  7.87 us
  transfers between devices with their start and end apart: 5, of which 3 were waited for; matrix products, arithmetic and copies ran while one was open for 4% of the time, Pallas kernels for 0%

profile of v1, /device:TPU:1, one launch (start us, length us, event | category | flops | bytes accessed | tf_op | source)
XLA Modules:
  0.0 293.5 jit_solution(16427295938624237186)
XLA Ops:
  7.2 0.0 copy-start
  7.2 0.0 copy-start.4
  7.2 0.0 all-reduce.4.cloned.1.call-start
  7.2 2.8 copy.37
  10.0 0.9 fusion.5
  11.0 4.0 %collective-permute-start = (bf16[3,256,192]{2,1,0:T(8,128)(2,1)}, bf16[3,256,192]{2,1,0:T(8,128)(2,1)S(1)}, u32[]{:S(2)}, u32[]{:S(2)}) collective-permute-start(bf16[3,256,192]{2,1,0:T(8,128)(2,1)} %get-tuple-element.16), channel_id=1, source_target_pairs={{0,4},{4,8},{8,12},{12,16},{16,20},{20,24},{24,28},{1,5},{5,9},{9,... | collective-permute-start | bytes 884744 | tf_op jit(solution)/shard_map/ppermute | solution.py:159
  15.0 1.3 collective-permute-start.1
  16.3 0.0 copy-done.4
  16.3 0.1 copy.42
  16.5 0.0 copy-start.5
  16.5 0.0 copy-start.3
  16.5 0.2 broadcast_select_fusion
  16.6 0.1 pad.13.clone
  16.7 1.9 pad_maximum_fusion.1.q_ref
  18.7 0.0 copy-done.5
  18.7 0.0 copy-start.7
  18.7 0.0 copy-start.6
  18.7 0.0 copy-start.8
  18.7 0.0 copy-start.9
  18.8 0.0 copy-done.3
  18.8 1.0 copy.43.wout_ref
  19.7 11.7 %collective-permute-done = bf16[3,256,192]{2,1,0:T(8,128)(2,1)S(1)} collective-permute-done((bf16[3,256,192]{2,1,0:T(8,128)(2,1)}, bf16[3,256,192]{2,1,0:T(8,128)(2,1)S(1)}, u32[]{:S(2)}, u32[]{:S(2)}) %collective-permute-start) | collective-permute-done | bytes 294944 | tf_op jit(solution)/shard_map/ppermute | solution.py:159
  31.4 0.0 collective-permute-done.1
  31.5 0.8 pad_maximum_fusion.5
  32.2 4.5 %collective-permute-start.2 = (bf16[22,16,192]{2,1,0:T(8,128)(2,1)}, bf16[22,16,192]{2,1,0:T(8,128)(2,1)S(1)}, u32[]{:S(2)}, u32[]{:S(2)}) collective-permute-start(bf16[22,16,192]{2,1,0:T(8,128)(2,1)} %get-tuple-element.14), channel_id=1, source_target_pairs={{0,1},{1,2},{2,3},{4,5},{5,6},{6,7},{8,9},{9,10},{10,11},{12,13},{... | collective-permute-start | bytes 405512 | tf_op jit(solution)/shard_map/ppermute | solution.py:159
  36.8 1.9 collective-permute-start.3
  38.7 0.7 fusion.3
  39.5 1.6 copy.41
  41.1 0.0 copy-done.7
  41.1 0.6 reshape.60.bin_ref
  41.7 0.7 pad.8.bias_ref
  42.4 0.0 copy-done.6
  42.4 0.0 copy-done.8
  42.4 0.0 copy-done.9
  42.4 1.3 stack.26.vec_ref
  43.7 0.0 collective-permute-done.2
  43.7 0.1 collective-permute-done.3
  43.8 2.0 pad_maximum_fusion.x_ref
  45.8 0.8 broadcast_in_dim.57.dw_ref
  46.6 59.8 %block.1 = (bf16[16,256,192]{2,1,0:T(8,128)(2,1)}, f32[512,256]{1,0:T(8,128)}) custom-call(bf16[22,288,192]{2,1,0:T(8,128)(2,1)} %pad_maximum_fusion.x_ref, bf16[16,4096]{1,0:T(8,128)(2,1)} %pad.8.bias_ref, f32[2,7,7,8,128]{4,3,2,1,0:T(8,128)} %broadcast_in_dim.57.dw_ref, f32[8,192]{1,0:T(8,128)} %stack.26.vec_ref, bf16[192,768]{1,0:T(8,128)(2,1)} %win_ref.1, ...), custom_call_target="tpu_custom_call" | custom-call | tf_op jit(solution)/shard_map/block/pallas_call | solution.py:202
  106.4 0.0 copy-start.1
  106.4 1.1 slice.32
  107.6 43.1 %pmax.7 = f32[512,8]{1,0:T(8,128)S(1)} all-reduce(f32[512,8]{1,0:T(8,128)S(1)} %slice.32), channel_id=1, replica_groups=mesh['row'=8,'col'=4] {'row','col'}, use_global_device_ids=true, to_apply=%region_0.1 | all-reduce | flops 4096 | bytes 32768 | tf_op jit(solution)/shard_map/pmax | solution.py:233
  150.7 0.0 copy-start.2
  150.7 1.4 slice_multiply_fusion.1
  152.1 0.1 copy.44
  152.2 0.8 broadcast_in_dim.64
  153.0 1.2 copy.45
  154.2 0.0 copy-done.1
  154.2 0.1 slice_multiply_fusion
  154.3 0.9 pad_maximum_fusion.2
  155.2 0.0 all-reduce.4.cloned.1.call-update
  155.3 0.0 copy-done.2
  155.3 2.3 copy.48
  157.5 125.6 %all-reduce.4.cloned.1.call-done = f32[512,200]{1,0:T(8,128)} async-done(((f32[512,200]{1,0:T(8,128)}), f32[512,200]{1,0:T(8,128)}) %all-reduce.4.cloned.1.call-update) | async-done | bytes 409616 | tf_op jit(solution)/shard_map/psum | solution.py:242
  283.2 1.1 slice.39
  284.3 0.1 copy.46
  284.4 0.2 copy.47
  284.6 0.0 copy-done
  284.6 2.1 fusion.1
  (8 shorter events, 0.1 us)
Async XLA Ops:
  7.2 277.4 %copy-start = (bf16[192,192]{1,0:T(8,128)(2,1)S(1)}, bf16[192,192]{1,0:T(8,128)(2,1)}, u32[]{:S(2)}) copy-start(bf16[192,192]{1,0:T(8,128)(2,1)} %param.29) | copy-start | bytes 221188
  7.2 9.1 %copy-start.4 = (bf16[512,192]{0,1:T(8,128)(2,1)S(1)}, bf16[512,192]{0,1:T(8,128)(2,1)}, u32[]{:S(2)}) copy-start(bf16[512,192]{0,1:T(8,128)(2,1)} %param.28) | copy-start | bytes 589828
  7.2 276.0 %all-reduce.4.cloned.1.call-start = ((), (), s32[]{:S(2)}) async-start(), calls=%async_computation | async-start | bytes 1048576 | tf_op jit(solution)/shard_map/psum | solution.py:242
  11.0 20.5 %collective-permute-start = (bf16[3,256,192]{2,1,0:T(8,128)(2,1)}, bf16[3,256,192]{2,1,0:T(8,128)(2,1)S(1)}, u32[]{:S(2)}, u32[]{:S(2)}) collective-permute-start(bf16[3,256,192]{2,1,0:T(8,128)(2,1)} %get-tuple-element.16), channel_id=1, source_target_pairs={{0,4},{4,8},{8,12},{12,16},{16,20},{20,24},{24,28},{1,5},{5,9},{9,... | collective-permute-start | bytes 884744 | tf_op jit(solution)/shard_map/ppermute | solution.py:159
  15.0 16.5 %collective-permute-start.1 = (bf16[3,256,192]{2,1,0:T(8,128)(2,1)}, bf16[3,256,192]{2,1,0:T(8,128)(2,1)S(1)}, u32[]{:S(2)}, u32[]{:S(2)}) collective-permute-start(bf16[3,256,192]{2,1,0:T(8,128)(2,1)} %get-tuple-element.17), channel_id=1, source_target_pairs={{4,0},{8,4},{12,8},{16,12},{20,16},{24,20},{28,24},{5,1},{9,5},{13... | collective-permute-start | bytes 884744 | tf_op jit(solution)/shard_map/ppermute | solution.py:160
  16.5 2.2 copy-start.5
  16.5 2.3 copy-start.3
  18.7 22.4 %copy-start.7 = (f32[768]{0:T(1024)S(1)}, f32[768]{0:T(1024)}, u32[]{:S(2)}) copy-start(f32[768]{0:T(1024)} %param.22) | copy-start | bytes 9220
  18.7 23.7 %copy-start.6 = (f32[192]{0:T(256)S(1)}, f32[192]{0:T(256)}, u32[]{:S(2)}) copy-start(f32[192]{0:T(256)} %param.24) | copy-start | bytes 2308
  18.7 23.7 %copy-start.8 = (f32[192]{0:T(256)S(1)}, f32[192]{0:T(256)}, u32[]{:S(2)}) copy-start(f32[192]{0:T(256)} %param.18) | copy-start | bytes 2308
  18.7 23.7 %copy-start.9 = (f32[192]{0:T(256)S(1)}, f32[192]{0:T(256)}, u32[]{:S(2)}) copy-start(f32[192]{0:T(256)} %param.19) | copy-start | bytes 2308
  32.2 11.4 %collective-permute-start.2 = (bf16[22,16,192]{2,1,0:T(8,128)(2,1)}, bf16[22,16,192]{2,1,0:T(8,128)(2,1)S(1)}, u32[]{:S(2)}, u32[]{:S(2)}) collective-permute-start(bf16[22,16,192]{2,1,0:T(8,128)(2,1)} %get-tuple-element.14), channel_id=1, source_target_pairs={{0,1},{1,2},{2,3},{4,5},{5,6},{6,7},{8,9},{9,10},{10,11},{12,13},{... | collective-permute-start | bytes 405512 | tf_op jit(solution)/shard_map/ppermute | solution.py:159
  36.8 7.0 %collective-permute-start.3 = (bf16[22,16,192]{2,1,0:T(8,128)(2,1)}, bf16[22,16,192]{2,1,0:T(8,128)(2,1)S(1)}, u32[]{:S(2)}, u32[]{:S(2)}) collective-permute-start(bf16[22,16,192]{2,1,0:T(8,128)(2,1)} %get-tuple-element.15), channel_id=1, source_target_pairs={{1,0},{2,1},{3,2},{5,4},{6,5},{7,6},{9,8},{10,9},{11,10},{13,12},{... | collective-permute-start | bytes 405512 | tf_op jit(solution)/shard_map/ppermute | solution.py:160
  106.4 47.8 %copy-start.1 = (f32[512,256]{1,0:T(8,128)S(1)}, f32[512,256]{1,0:T(8,128)}, u32[]{:S(2)}) copy-start(f32[512,256]{1,0:T(8,128)} %get-tuple-element.5) | copy-start | bytes 1572868
  150.7 4.5 %copy-start.2 = (bf16[16,256,192]{2,1,0:T(8,128)(2,1)S(1)}, bf16[16,256,192]{2,1,0:T(8,128)(2,1)}, u32[]{:S(2)}) copy-start(bf16[16,256,192]{2,1,0:T(8,128)(2,1)} %get-tuple-element.10) | copy-start | bytes 4718596
Sparse Core Ops, SparseCore 0:
  155.4 127.7 all-reduce.3

commit v2 on v1

--- a/solution.py
+++ b/solution.py
@@ -148,6 +148,140 @@
         return top_a
 
     lax.fori_loop(0, total // 2, attend, top_a)
+
+
+MESH = pl.DeviceIdType.MESH
+
+
+def join(packed, owner, low, high):
+    top = packed[0]
+    for other in packed[1:]:
+        top = jnp.maximum(top, other)
+    total = None
+    for piece in packed:
+        keep = jnp.exp2(piece - top)
+        factor = jnp.ones_like(piece)
+        for head in range(NH):
+            factor = jnp.where(owner == head, keep[:, high + head : high + head + 1], factor)
+        term = piece * factor
+        total = term if total is None else total + term
+    lane = lax.broadcasted_iota(jnp.int32, total.shape, 1)
+    return jnp.where(lane >= high, top, total)
+
+
+def owners(shape, channels):
+    lane = lax.broadcasted_iota(jnp.int32, shape, 1)
+    return jnp.where(
+        lane < channels,
+        lane // (channels // NH),
+        jnp.where(lane < channels + NH, lane - channels, NH),
+    )
+
+
+def merge_kernel(
+    nr,
+    nc,
+    channels,
+    part_ref,
+    out_ref,
+    col_buf,
+    mid,
+    row_buf,
+    gathered,
+    send_1,
+    recv_1,
+    send_2,
+    recv_2,
+    send_3,
+    recv_3,
+    send_4,
+    recv_4,
+):
+    r, c = lax.axis_index("row"), lax.axis_index("col")
+    count_r = part_ref.shape[1] // nr
+    barrier = pltpu.get_barrier_semaphore()
+    for k in range(1, nc):
+        pl.semaphore_signal(
+            barrier, inc=1, device_id=(r, lax.rem(c + k, nc)), device_id_type=MESH
+        )
+    for k in range(1, nr):
+        pl.semaphore_signal(
+            barrier, inc=1, device_id=(lax.rem(r + k, nr), c), device_id_type=MESH
+        )
+    pl.semaphore_wait(barrier, nc + nr - 2)
+
+    def spread(src, dst, send, recv, count, along_col):
+        copies = []
+        for k in range(1, count):
+            peer = lax.rem((c if along_col else r) + k, count)
+            copy = pltpu.make_async_remote_copy(
+                src_ref=src(peer),
+                dst_ref=dst(k),
+                send_sem=send.at[k - 1],
+                recv_sem=recv.at[k - 1],
+                device_id=(r, peer) if along_col else (peer, c),
+                device_id_type=MESH,
+            )
+            copy.start()
+            copies.append(copy)
+        return copies
+
+    low, high = channels, channels + NH
+    first = spread(lambda p: part_ref.at[p], lambda k: col_buf.at[k - 1], send_1, recv_1, nc, True)
+    for copy in first:
+        copy.wait()
+    owner = owners(part_ref.shape[1:], channels)
+    pieces = [part_ref[c]] + [col_buf[k] for k in range(nc - 1)]
+    total = join(pieces, owner, low, high)
+    for j in range(nr):
+        mid[j] = total[j * count_r : (j + 1) * count_r]
+    second = spread(lambda p: mid.at[p], lambda k: row_buf.at[k - 1], send_2, recv_2, nr, False)
+    for copy in second:
+        copy.wait()
+    owner = owners(mid.shape[1:], channels)
+    pieces = [mid[r]] + [row_buf[k] for k in range(nr - 1)]
+    total = join(pieces, owner, low, high)
+    divisor = jnp.ones_like(total)
+    for head in range(NH):
+        divisor = jnp.where(owner == head, total[:, low + head : low + head + 1], divisor)
+    pooled = total / divisor
+    gathered[c, r] = pooled[:, 0:channels].astype(jnp.bfloat16)
+    third = spread(
+        lambda p: gathered.at[c, r], lambda k: gathered.at[c, r], send_3, recv_3, nr, False
+    )
+    for copy in third:
+        copy.wait()
+    fourth = spread(lambda p: gathered.at[c], lambda k: gathered.at[c], send_4, recv_4, nc, True)
+    for copy in fourth:
+        copy.wait()
+    out_ref[...] = gathered[...]
+
+
+def merged(part, channels):
+    nr, nc = lax.axis_size("row"), lax.axis_size("col")
+    count_c = part.shape[0] // nc
+    count_r = count_c // nr
+    wide = part.shape[1]
+    whole = pl.BlockSpec(memory_space=pltpu.VMEM)
+    sems = []
+    for n in (nc, nr, nr, nc):
+        sems += [pltpu.SemaphoreType.DMA((n - 1,))] * 2
+    pooled = pl.pallas_call(
+        functools.partial(merge_kernel, nr, nc, channels),
+        out_shape=jax.ShapeDtypeStruct((nc, nr, count_r, channels), jnp.bfloat16),
+        in_specs=[whole],
+        out_specs=whole,
+        scratch_shapes=[
+            pltpu.VMEM((nc - 1, count_c, wide), jnp.float32),
+            pltpu.VMEM((nr, count_r, wide), jnp.float32),
+            pltpu.VMEM((nr - 1, count_r, wide), jnp.float32),
+            pltpu.VMEM((nc, nr, count_r, channels), jnp.bfloat16),
+        ]
+        + sems,
+        compiler_params=pltpu.CompilerParams(collective_id=0, has_side_effects=True),
+        name="merge",
+    )(part.reshape(nc, count_c, wide))
+    return pooled.reshape(part.shape[0], channels)
 
 
 def halo(value, axis, dim, width):
@@ -229,20 +363,8 @@
         w_value,
         q_wide,
     )
-    top = part[:, channels + NH : channels + 2 * NH]
-    best = lax.pmax(top, ("row", "col"))
-    keep = jnp.exp2(top - best)
-    scaled = jnp.concatenate(
-        [
-            part[:, :channels] * jnp.repeat(keep, head_size, axis=1),
-            part[:, channels : channels + NH] * keep,
-        ],
-        axis=1,
-    )
-    merged = lax.psum(scaled, ("row", "col"))
-    pooled = merged[:, :channels] / jnp.repeat(merged[:, channels:], head_size, axis=1)
     pooled_out = jnp.dot(
-        pooled.astype(jnp.bfloat16), w_proj, preferred_element_type=jnp.float32
+        merged(part, channels), w_proj, preferred_element_type=jnp.float32
     )
     return (block_out, pooled_out)
 

time: 296 us -> 134 us (0.45)
  waiting for transfers between devices: 138 us -> 11.9 us
  blocking collectives: 43.1 us -> 0 us
  Pallas kernels: 59.8 us -> 87.3 us
  between operations: 14.3 us -> 0.82 us
  local copies, waits for them, and re-layouts: 16.9 us -> 13.9 us
    psum x1 -> x0, waiting for transfers between devices: 126 us -> none  [body(): merged = lax.psum(scaled, ('row', 'col'))]
    pmax x1 -> x0, blocking collectives: 43.1 us -> none  [body(): best = lax.pmax(top, ('row', 'col'))]
    pallas_call x0 -> x1, Pallas kernels: none -> 27.4 us  [merged(): pl.pallas_call(functools.partial(merge_kernel, nr, nc, channels), out_sha...]
    unnamed x26 -> x22, local copies, waits for them, and re-layouts: 7.87 us -> 9.49 us
  transfers between devices with their start and end apart: 5 -> 4, of which waited for: 3 -> 2; matrix products, arithmetic and copies ran while one was open for 4% -> 6% of each run, Pallas kernels for 0% -> 0%
where the time goes in v2:
time: 134 us; the launch traced here: 133 us
  Pallas kernels  87.3 us (65%)
  local copies, waits for them, and re-layouts  13.9 us (10%)
  waiting for transfers between devices  11.9 us (9%)
  starting transfers between devices  11.7 us (9%)
  other arithmetic  5.66 us (4%)
  matrix products  1.95 us (1%)
    pallas_call x1, Pallas kernels, body(): pl.pallas_call(functools.partial(block_kernel, rows, cols, channels, hidd...  59.8 us
    pallas_call x1, Pallas kernels, merged(): pl.pallas_call(functools.partial(merge_kernel, nr, nc, channels), out_sha...  27.4 us
    ppermute x2, waiting for transfers between devices, halo(): before = lax.ppermute(last, axis, up)  11.7 us
    unnamed x22, local copies, waits for them, and re-layouts  9.49 us
    ppermute x2, starting transfers between devices, halo(): before = lax.ppermute(last, axis, up)  8.52 us
    ppermute x2, starting transfers between devices, halo(): after = lax.ppermute(initial, axis, down)  3.21 us
  transfers between devices with their start and end apart: 4, of which 2 were waited for; matrix products, arithmetic and copies ran while one was open for 6% of the time, Pallas kernels for 0%

profile of v2, /device:TPU:1, one launch (start us, length us, event | category | flops | bytes accessed | tf_op | source)
XLA Modules:
  0.0 133.1 jit_solution(2594544622954675426)
XLA Ops:
  0.6 0.0 copy-start
  0.6 0.0 copy-start.2
  0.7 2.8 %copy.17 = bf16[16,256,192]{2,1,0:T(8,128)(2,1)S(1)} copy(bf16[16,256,192]{1,2,0:T(8,128)(2,1)} %param.15) | data formatting | bytes 3145728 | tf_op args[0]
  3.5 0.9 fusion.2
  4.4 4.0 %collective-permute-start = (bf16[3,256,192]{2,1,0:T(8,128)(2,1)}, bf16[3,256,192]{2,1,0:T(8,128)(2,1)S(1)}, u32[]{:S(2)}, u32[]{:S(2)}) collective-permute-start(bf16[3,256,192]{2,1,0:T(8,128)(2,1)} %get-tuple-element.10), channel_id=1, source_target_pairs={{0,4},{4,8},{8,12},{12,16},{16,20},{20,24},{24,28},{1,5},{5,9},{9,... | collective-permute-start | bytes 884744 | tf_op jit(solution)/shard_map/ppermute | solution.py:293
  8.4 1.3 collective-permute-start.1
  9.7 0.0 copy-done.2
  9.7 0.1 copy.22
  9.9 0.0 copy-start.3
  9.9 0.0 copy-start.1
  9.9 0.2 broadcast_select_fusion
  10.1 0.1 pad.11.clone
  10.1 1.9 %pad_maximum_fusion.1.q_ref = bf16[4096,208]{1,0:T(8,128)(2,1)} fusion(bf16[4096,192]{1,0:T(8,128)(2,1)S(1)} %bitcast.18, bf16[208]{0:T(256)(128)(2,1)S(1)} %pad.11.clone), kind=kLoop, calls=%fused_computation.1 | loop fusion | flops 3407872 | bytes 3277216 | tf_op jit(solution)/shard_map/concatenate | solution.py:333
  12.1 0.0 copy-done.3
  12.1 0.0 copy-start.5
  12.1 0.0 copy-start.4
  12.1 0.0 copy-start.6
  12.1 0.0 copy-start.7
  12.2 0.0 copy-done.1
  12.2 1.0 copy.23.wout_ref
  13.2 11.7 %collective-permute-done = bf16[3,256,192]{2,1,0:T(8,128)(2,1)S(1)} collective-permute-done((bf16[3,256,192]{2,1,0:T(8,128)(2,1)}, bf16[3,256,192]{2,1,0:T(8,128)(2,1)S(1)}, u32[]{:S(2)}, u32[]{:S(2)}) %collective-permute-start) | collective-permute-done | bytes 294944 | tf_op jit(solution)/shard_map/ppermute | solution.py:293
  24.9 0.0 collective-permute-done.1
  24.9 0.8 pad_maximum_fusion.4
  25.7 4.5 %collective-permute-start.2 = (bf16[22,16,192]{2,1,0:T(8,128)(2,1)}, bf16[22,16,192]{2,1,0:T(8,128)(2,1)S(1)}, u32[]{:S(2)}, u32[]{:S(2)}) collective-permute-start(bf16[22,16,192]{2,1,0:T(8,128)(2,1)} %get-tuple-element.8), channel_id=1, source_target_pairs={{0,1},{1,2},{2,3},{4,5},{5,6},{6,7},{8,9},{9,10},{10,11},{12,13},{... | collective-permute-start | bytes 405512 | tf_op jit(solution)/shard_map/ppermute | solution.py:293
  30.2 1.9 %collective-permute-start.3 = (bf16[22,16,192]{2,1,0:T(8,128)(2,1)}, bf16[22,16,192]{2,1,0:T(8,128)(2,1)S(1)}, u32[]{:S(2)}, u32[]{:S(2)}) collective-permute-start(bf16[22,16,192]{2,1,0:T(8,128)(2,1)} %get-tuple-element.9), channel_id=1, source_target_pairs={{1,0},{2,1},{3,2},{5,4},{6,5},{7,6},{9,8},{10,9},{11,10},{13,12},{... | collective-permute-start | bytes 405512 | tf_op jit(solution)/shard_map/ppermute | solution.py:294
  32.1 0.7 fusion
  32.9 1.6 %copy.21 = bf16[192,192]{0,1:T(8,128)(2,1)} copy(bf16[192,192]{1,0:T(8,128)(2,1)} %param.26) | data formatting | bytes 147456 | tf_op args[11]
  34.5 0.0 copy-done.5
  34.5 0.6 reshape.60.bin_ref
  35.1 0.7 pad.8.bias_ref
  35.8 0.0 copy-done.4
  35.8 0.0 copy-done.6
  35.8 0.0 copy-done.7
  35.8 1.3 stack.26.vec_ref
  37.1 0.0 collective-permute-done.2
  37.1 0.1 collective-permute-done.3
  37.2 2.0 %pad_maximum_fusion.x_ref = bf16[22,288,192]{2,1,0:T(8,128)(2,1)} fusion(bf16[22,16,192]{2,1,0:T(8,128)(2,1)S(1)} %collective-permute-done.3, bf16[3,256,192]{2,1,0:T(8,128)(2,1)S(1)} %collective-permute-done.1, bf16[16,256,192]{2,1,0:T(8,128)(2,1)S(1)} %copy.17, bf16[3,256,192]{2,1,0:T(8,128)(2,1)S(1)} %collective-permute-done, ...), kind=kLoop, calls=%fused_computation | loop fusion | flops 12165120 | bytes 4866048 | tf_op jit(solution)/shard_map/concatenate | solution.py:295
  39.3 0.8 broadcast_in_dim.51.dw_ref
  40.0 59.8 %block.1 = (bf16[16,256,192]{2,1,0:T(8,128)(2,1)}, f32[512,256]{1,0:T(8,128)}) custom-call(bf16[22,288,192]{2,1,0:T(8,128)(2,1)} %pad_maximum_fusion.x_ref, bf16[16,4096]{1,0:T(8,128)(2,1)} %pad.8.bias_ref, f32[2,7,7,8,128]{4,3,2,1,0:T(8,128)} %broadcast_in_dim.51.dw_ref, f32[8,192]{1,0:T(8,128)} %stack.26.vec_ref, bf16[192,768]{1,0:T(8,128)(2,1)} %win_ref.1, ...), custom_call_target="tpu_custom_call" | custom-call | tf_op jit(solution)/shard_map/block/pallas_call | solution.py:336
  99.9 3.9 %copy.24 = bf16[16,256,192]{1,2,0:T(8,128)(2,1)} copy(bf16[16,256,192]{2,1,0:T(8,128)(2,1)} %get-tuple-element.6) | data formatting | bytes 3145728
  103.7 27.4 %merge.1 = bf16[4,8,16,192]{3,2,1,0:T(8,128)(2,1)} custom-call(f32[4,128,256]{2,1,0:T(8,128)} %bitcast.20), custom_call_target="tpu_custom_call" | custom-call | tf_op jit(solution)/shard_map/merge/pallas_call | solution.py:269
  131.2 0.0 copy-done
  131.2 1.9 %fusion.3 = f32[512,192]{0,1:T(8,128)} fusion(bf16[512,192]{1,0:T(8,128)(2,1)} %bitcast.19, bf16[192,192]{1,0:T(8,128)(2,1)S(1)} %copy-done), kind=kOutput, calls=%fused_computation.17 | convolution fusion | flops 37748736 | bytes 663552 | tf_op jit(solution)/shard_map/dot_general | solution.py:366
  (7 shorter events, 0.1 us)
Async XLA Ops:
  0.6 130.6 %copy-start = (bf16[192,192]{1,0:T(8,128)(2,1)S(1)}, bf16[192,192]{1,0:T(8,128)(2,1)}, u32[]{:S(2)}) copy-start(bf16[192,192]{1,0:T(8,128)(2,1)} %param.29) | copy-start | bytes 221188
  0.6 9.1 %copy-start.2 = (bf16[512,192]{0,1:T(8,128)(2,1)S(1)}, bf16[512,192]{0,1:T(8,128)(2,1)}, u32[]{:S(2)}) copy-start(bf16[512,192]{0,1:T(8,128)(2,1)} %param.28) | copy-start | bytes 589828
  4.4 20.5 %collective-permute-start = (bf16[3,256,192]{2,1,0:T(8,128)(2,1)}, bf16[3,256,192]{2,1,0:T(8,128)(2,1)S(1)}, u32[]{:S(2)}, u32[]{:S(2)}) collective-permute-start(bf16[3,256,192]{2,1,0:T(8,128)(2,1)} %get-tuple-element.10), channel_id=1, source_target_pairs={{0,4},{4,8},{8,12},{12,16},{16,20},{20,24},{24,28},{1,5},{5,9},{9,... | collective-permute-start | bytes 884744 | tf_op jit(solution)/shard_map/ppermute | solution.py:293
  8.4 16.5 %collective-permute-start.1 = (bf16[3,256,192]{2,1,0:T(8,128)(2,1)}, bf16[3,256,192]{2,1,0:T(8,128)(2,1)S(1)}, u32[]{:S(2)}, u32[]{:S(2)}) collective-permute-start(bf16[3,256,192]{2,1,0:T(8,128)(2,1)} %get-tuple-element.11), channel_id=1, source_target_pairs={{4,0},{8,4},{12,8},{16,12},{20,16},{24,20},{28,24},{5,1},{9,5},{13... | collective-permute-start | bytes 884744 | tf_op jit(solution)/shard_map/ppermute | solution.py:294
  9.9 2.2 %copy-start.3 = (f32[7,7,192]{2,1,0:T(8,128)S(1)}, f32[7,7,192]{2,1,0:T(8,128)}, u32[]{:S(2)}) copy-start(f32[7,7,192]{2,1,0:T(8,128)} %param.17) | copy-start | bytes 112900
  9.9 2.3 %copy-start.1 = (bf16[768,192]{0,1:T(8,128)(2,1)S(1)}, bf16[768,192]{0,1:T(8,128)(2,1)}, u32[]{:S(2)}) copy-start(bf16[768,192]{0,1:T(8,128)(2,1)} %param.23) | copy-start | bytes 884740
  12.1 22.4 %copy-start.5 = (f32[768]{0:T(1024)S(1)}, f32[768]{0:T(1024)}, u32[]{:S(2)}) copy-start(f32[768]{0:T(1024)} %param.22) | copy-start | bytes 9220
  12.1 23.7 %copy-start.4 = (f32[192]{0:T(256)S(1)}, f32[192]{0:T(256)}, u32[]{:S(2)}) copy-start(f32[192]{0:T(256)} %param.24) | copy-start | bytes 2308
  12.1 23.7 %copy-start.6 = (f32[192]{0:T(256)S(1)}, f32[192]{0:T(256)}, u32[]{:S(2)}) copy-start(f32[192]{0:T(256)} %param.18) | copy-start | bytes 2308
  12.1 23.7 %copy-start.7 = (f32[192]{0:T(256)S(1)}, f32[192]{0:T(256)}, u32[]{:S(2)}) copy-start(f32[192]{0:T(256)} %param.19) | copy-start | bytes 2308
  25.7 11.4 %collective-permute-start.2 = (bf16[22,16,192]{2,1,0:T(8,128)(2,1)}, bf16[22,16,192]{2,1,0:T(8,128)(2,1)S(1)}, u32[]{:S(2)}, u32[]{:S(2)}) collective-permute-start(bf16[22,16,192]{2,1,0:T(8,128)(2,1)} %get-tuple-element.8), channel_id=1, source_target_pairs={{0,1},{1,2},{2,3},{4,5},{5,6},{6,7},{8,9},{9,10},{10,11},{12,13},{... | collective-permute-start | bytes 405512 | tf_op jit(solution)/shard_map/ppermute | solution.py:293
  30.2 7.0 %collective-permute-start.3 = (bf16[22,16,192]{2,1,0:T(8,128)(2,1)}, bf16[22,16,192]{2,1,0:T(8,128)(2,1)S(1)}, u32[]{:S(2)}, u32[]{:S(2)}) collective-permute-start(bf16[22,16,192]{2,1,0:T(8,128)(2,1)} %get-tuple-element.9), channel_id=1, source_target_pairs={{1,0},{2,1},{3,2},{5,4},{6,5},{7,6},{9,8},{10,9},{11,10},{13,12},{... | collective-permute-start | bytes 405512 | tf_op jit(solution)/shard_map/ppermute | solution.py:294

commit v3 on v2

--- a/solution.py
+++ b/solution.py
@@ -21,17 +21,28 @@
     hidden,
     query_count,
     x_ref,
+    above_ref,
+    below_ref,
+    left_ref,
+    right_ref,
     bias_ref,
-    dw_ref,
-    vec_ref,
+    dw_raw_ref,
+    dw_bias_ref,
+    gain_ref,
+    shift_ref,
+    b_out_ref,
+    scale_ref,
     win_ref,
     bin_ref,
     wout_ref,
-    wkt_ref,
+    wk_ref,
     wv_ref,
-    q_ref,
+    q_raw_ref,
     out_ref,
     part_ref,
+    dw_ref,
+    q_ref,
+    wkt_ref,
     xf_ref,
     conv_ref,
     kt_ref,
@@ -45,13 +56,41 @@
     wide = 256
     high = channels - 128
 
+    def place(i, start, size, line):
+        line = line.astype(jnp.float32)
+        xf_ref[0, i, start : start + size] = line[:, 0:128]
+        xf_ref[1, i, start : start + size, 0:high] = line[:, 128:channels]
+
     def widen(i, carry):
-        line = x_ref[i].astype(jnp.float32)
-        xf_ref[0, i] = line[:, 0:128]
-        xf_ref[1, i, :, 0:high] = line[:, 128:channels]
+        place(i + 3, PAD, cols, x_ref[i])
         return carry
 
-    lax.fori_loop(0, rows + 6, widen, 0)
+    def sides(i, carry):
+        place(i, 0, PAD, left_ref[i])
+        place(i, PAD + cols, PAD, right_ref[i])
+        return carry
+
+    lax.fori_loop(0, rows, widen, 0)
+    lax.fori_loop(0, rows + 6, sides, 0)
+    for i in range(3):
+        place(i, PAD, cols, above_ref[i])
+        place(rows + 3 + i, PAD, cols, below_ref[i])
+    for i in range(7):
+        for j in range(7):
+            dw_ref[0, i, j] = jnp.broadcast_to(dw_raw_ref[i, j : j + 1, 0:128], (8, 128))
+            dw_ref[1, i, j, :, 0:high] = jnp.broadcast_to(
+                dw_raw_ref[i, j : j + 1, 128:channels], (8, high)
+            )
+    wkt_ref[...] = jnp.transpose(wk_ref[...].astype(jnp.float32)).astype(jnp.bfloat16)
+    q_lane = lax.broadcasted_iota(jnp.int32, (query_count, channels), 1) // head_size
+    tail_lane = lax.broadcasted_iota(jnp.int32, (query_count, depth - channels), 1)
+    q_tail = jnp.where(tail_lane == 0, 1.0, 0.0).astype(jnp.bfloat16)
+    q_all = q_raw_ref[...].astype(jnp.float32)
+    for head in range(NH):
+        at = head * query_count
+        own = jnp.where(q_lane == head, q_all, 0.0).astype(jnp.bfloat16)
+        q_ref[at : at + query_count, 0:channels] = own
+        q_ref[at : at + query_count, channels:depth] = q_tail
 
     def conv_tile(tile, carry):
         start = pl.multiple_of(tile * 8, 8)
@@ -73,11 +112,12 @@
     lax.fori_loop(0, cols // 8, conv_tile, 0)
 
     block = 2 * cols
-    dw_bias = vec_ref[0:1, :]
-    gain = vec_ref[1:2, :]
-    shift = vec_ref[2:3, :]
-    b_out = vec_ref[3:4, :]
-    scale = vec_ref[4:5, :]
+    dw_bias = dw_bias_ref[...][None, :]
+    gain = gain_ref[...][None, :]
+    shift = shift_ref[...][None, :]
+    b_out = b_out_ref[...][None, :]
+    scale = scale_ref[...][None, :]
+    b_in = bin_ref[...][None, :]
     kt_ref[channels:depth, :] = jnp.zeros((depth - channels, positions), jnp.bfloat16)
     kt_ref[channels : channels + 16, :] = bias_ref[...]
     lane16 = lax.broadcasted_iota(jnp.int32, (positions, wide - channels), 1)
@@ -86,16 +126,19 @@
     def mlp(step, carry):
         row = step * 2
         flat = conv_ref[pl.ds(row, 2)].reshape(block, wide)[:, 0:channels] + dw_bias
-        center = x_ref[pl.ds(row + 3, 2), PAD : PAD + cols, :].reshape(block, channels)
+        center = x_ref[pl.ds(row, 2)].reshape(block, channels)
         average = jnp.mean(flat, axis=-1, keepdims=True)
         moved = flat - average
         spread = jnp.mean(moved * moved, axis=-1, keepdims=True)
         normed = (moved * lax.rsqrt(spread + 1e-06) * gain + shift).astype(jnp.bfloat16)
-        inner = jnp.dot(normed, win_ref[...], preferred_element_type=jnp.float32) + bin_ref[...]
+        inner = jnp.dot(normed, win_ref[...], preferred_element_type=jnp.float32) + b_in
         act = (0.5 * inner * (1.0 + lax.erf(inner * math.sqrt(0.5)))).astype(jnp.bfloat16)
         branch = jnp.dot(act, wout_ref[...], preferred_element_type=jnp.float32) + b_out
-        result = (center.astype(jnp.float32) + scale * branch).astype(jnp.bfloat16)
-        out_ref[pl.ds(row, 2)] = result.reshape(2, cols, channels)
+        summed = center.astype(jnp.float32) + scale * branch
+        result = summed.astype(jnp.bfloat16)
+        for i in range(2):
+            line = jnp.transpose(summed[i * cols : (i + 1) * cols])
+            out_ref[row + i] = line.astype(jnp.bfloat16)
         first = pl.multiple_of(step * block, block)
         kt_ref[0:channels, pl.ds(first, block)] = lax.dot_general(
             wkt_ref[...], result, (((1,), (1,)), ((), ())), preferred_element_type=jnp.float32
@@ -284,15 +327,110 @@
     return pooled.reshape(part.shape[0], channels)
 
 
-def halo(value, axis, dim, width):
-    count, length = (lax.axis_size(axis), value.shape[dim])
-    up = [(i, i + 1) for i in range(count - 1)]
-    down = [(j, i) for i, j in up]
-    last = lax.slice_in_dim(value, length - width, length, axis=dim)
-    initial = lax.slice_in_dim(value, 0, width, axis=dim)
-    before = lax.ppermute(last, axis, up)
-    after = lax.ppermute(initial, axis, down)
-    return jnp.concatenate([before, value, after], axis=dim)
+SIDES = [(-1, 0), (1, 0), (0, -1), (0, 1), (-1, -1), (-1, 1), (1, -1), (1, 1)]
+
+
+def halo_kernel(
+    nr,
+    nc,
+    x_ref,
+    above_out,
+    below_out,
+    left_out,
+    right_out,
+    above,
+    below,
+    left,
+    right,
+    send,
+    recv,
+):
+    r, c = lax.axis_index("row"), lax.axis_index("col")
+    rows, cols = x_ref.shape[0], x_ref.shape[1]
+
+    def inside(dr, dc):
+        return (r + dr >= 0) & (r + dr < nr) & (c + dc >= 0) & (c + dc < nc)
+
+    barrier = pltpu.get_barrier_semaphore()
+    count = 0
+    for dr, dc in SIDES:
+        valid = inside(dr, dc)
+        count = count + jnp.where(valid, 1, 0)
+
+        @pl.when(valid)
+        def _(dr=dr, dc=dc):
+            pl.semaphore_signal(barrier, inc=1, device_id=(r + dr, c + dc), device_id_type=MESH)
+
+    pl.semaphore_wait(barrier, count)
+
+    def source(dr, dc):
+        at = {-1: pl.ds(0, 3), 0: pl.ds(0, rows), 1: pl.ds(rows - 3, 3)}[dr]
+        to = {-1: pl.ds(0, PAD), 0: pl.ds(0, cols), 1: pl.ds(cols - PAD, PAD)}[dc]
+        return x_ref.at[at, to]
+
+    def target(dr, dc):
+        if dc == 0:
+            return below if dr < 0 else above
+        strip = right if dc < 0 else left
+        at = {-1: pl.ds(rows + 3, 3), 0: pl.ds(3, rows), 1: pl.ds(0, 3)}[dr]
+        return strip.at[at]
+
+    def copy(d):
+        dr, dc = SIDES[d]
+        return pltpu.make_async_remote_copy(
+            src_ref=source(dr, dc),
+            dst_ref=target(dr, dc),
+            send_sem=send.at[d],
+            recv_sem=recv.at[d],
+            device_id=(r + dr, c + dc),
+            device_id_type=MESH,
+        )
+
+    for d, (dr, dc) in enumerate(SIDES):
+
+        @pl.when(inside(dr, dc))
+        def _(d=d):
+            copy(d).start()
+
+    for d, (dr, dc) in enumerate(SIDES):
+
+        @pl.when(jnp.logical_not(inside(-dr, -dc)))
+        def _(dr=dr, dc=dc):
+            place = target(dr, dc)
+            place[...] = jnp.zeros(place.shape, place.dtype)
+
+    for d, (dr, dc) in enumerate(SIDES):
+
+        @pl.when(inside(-dr, -dc))
+        def _(d=d):
+            copy(d).wait_recv()
+
+    above_out[...] = above[...]
+    below_out[...] = below[...]
+    left_out[...] = left[...]
+    right_out[...] = right[...]
+    for d, (dr, dc) in enumerate(SIDES):
+
+        @pl.when(inside(dr, dc))
+        def _(d=d):
+            copy(d).wait_send()
+
+
+def halo(feature):
+    nr, nc = lax.axis_size("row"), lax.axis_size("col")
+    rows, cols, channels = feature.shape
+    whole = pl.BlockSpec(memory_space=pltpu.VMEM)
+    shapes = [(3, cols, channels)] * 2 + [(rows + 6, PAD, channels)] * 2
+    return pl.pallas_call(
+        functools.partial(halo_kernel, nr, nc),
+        out_shape=[jax.ShapeDtypeStruct(shape, feature.dtype) for shape in shapes],
+        in_specs=[whole],
+        out_specs=[whole] * 4,
+        scratch_shapes=[pltpu.VMEM(shape, feature.dtype) for shape in shapes]
+        + [pltpu.SemaphoreType.DMA((8,)), pltpu.SemaphoreType.DMA((8,))],
+        compiler_params=pltpu.CompilerParams(collective_id=1, has_side_effects=True),
+        name="halo",
+    )(feature)
 
 
 def body(
@@ -316,32 +454,24 @@
     positions = rows * cols
     hidden = w_in.shape[1]
     query_count = queries.shape[0]
-    head_size = channels // NH
     depth = channels + 16
-    padded = halo(halo(feature, "row", 0, 3), "col", 1, PAD)
+    above, below, left, right = halo(feature)
     bias = jnp.where(mask > 0, 0.0, MASKED).astype(jnp.bfloat16).reshape(1, positions)
     bias = jnp.pad(bias, ((0, 15), (0, 0)))
-    dw = jnp.pad(dw_weight, ((0, 0), (0, 0), (0, 256 - channels)))
-    dw = jnp.transpose(dw.reshape(7, 7, 2, 128), (2, 0, 1, 3))
-    dw = jnp.broadcast_to(dw[:, :, :, None, :], (2, 7, 7, 8, 128))
-    vectors = jnp.stack([dw_bias, ln_gain, ln_bias, b_out, layer_scale] + [b_out] * 3)
-    channel_head = jnp.arange(channels) // head_size
-    own = channel_head[None, :] == jnp.arange(NH)[:, None]
-    spread = jnp.where(own[:, None, :], queries[None], 0).astype(jnp.bfloat16)
-    tail = jnp.where(jnp.arange(depth - channels) == 0, 1.0, 0.0).astype(jnp.bfloat16)
-    tail = jnp.broadcast_to(tail, (NH, query_count, depth - channels))
-    q_wide = jnp.concatenate([spread, tail], axis=-1).reshape(NH * query_count, depth)
     qb = 256
     whole = pl.BlockSpec(memory_space=pltpu.VMEM)
     block_out, part = pl.pallas_call(
         functools.partial(block_kernel, rows, cols, channels, hidden, query_count),
         out_shape=(
-            jax.ShapeDtypeStruct(feature.shape, jnp.bfloat16),
+            jax.ShapeDtypeStruct((rows, channels, cols), jnp.bfloat16),
             jax.ShapeDtypeStruct((query_count, 256), jnp.float32),
         ),
-        in_specs=[whole] * 10,
+        in_specs=[whole] * 18,
         out_specs=(whole, whole),
         scratch_shapes=[
+            pltpu.VMEM((2, 7, 7, 8, 128), jnp.float32),
+            pltpu.VMEM((NH * query_count, depth), jnp.bfloat16),
+            pltpu.VMEM((channels, channels), jnp.bfloat16),
             pltpu.VMEM((2, rows + 6, cols + 2 * PAD, 128), jnp.float32),
             pltpu.VMEM((rows, cols, 256), jnp.float32),
             pltpu.VMEM((depth, positions), jnp.bfloat16),
@@ -352,21 +482,29 @@
         compiler_params=pltpu.CompilerParams(vmem_limit_bytes=56 << 20),
         name="block",
     )(
-        padded,
+        feature,
+        above,
+        below,
+        left,
+        right,
         bias,
-        dw,
-        vectors,
+        dw_weight,
+        dw_bias,
+        ln_gain,
+        ln_bias,
+        b_out,
+        layer_scale,
         w_in,
-        b_in.reshape(1, hidden),
+        b_in,
         w_out,
-        jnp.transpose(w_key),
+        w_key,
         w_value,
-        q_wide,
+        queries,
     )
     pooled_out = jnp.dot(
         merged(part, channels), w_proj, preferred_element_type=jnp.float32
     )
-    return (block_out, pooled_out)
+    return (jnp.transpose(block_out, (0, 2, 1)), pooled_out)
 
 
 def solution(mesh):

time: 134 us -> 124 us (0.925)
  Pallas kernels: 87.3 us -> 112 us
  waiting for transfers between devices: 11.9 us -> 0 us
  starting transfers between devices: 11.7 us -> 0 us
  local copies, waits for them, and re-layouts: 13.9 us -> 8.06 us
  other arithmetic: 5.66 us -> 0.76 us
    pallas_call x0 -> x1, Pallas kernels: none -> 24.9 us  [halo(): pl.pallas_call(functools.partial(halo_kernel, nr, nc), out_shape=[jax.Sha...]
    ppermute x4 -> x0, waiting for transfers between devices: 11.9 us -> none  [the longest x2 11.7 us: halo(): before = lax.ppermute(last, axis, up)]
    ppermute x4 -> x0, starting transfers between devices: 11.7 us -> none  [the longest x2 8.52 us: halo(): before = lax.ppermute(last, axis, up)]
    concatenate x2 -> x0, other arithmetic: 3.97 us -> none  [the longest x1 2.02 us: halo(): return jnp.concatenate([before, value, after], axis=dim)]
    unnamed x22 -> x6, local copies, waits for them, and re-layouts: 9.49 us -> 7.39 us
  transfers between devices with their start and end apart: 4 -> 0, of which waited for: 2 -> 0; matrix products, arithmetic and copies ran while one was open for 6% -> 0% of each run, Pallas kernels for 0% -> 0%
where the time goes in v3:
time: 124 us
  Pallas kernels  112 us (90%)
  local copies, waits for them, and re-layouts  8.06 us (6%)
  matrix products  1.95 us (2%)
    pallas_call x1, Pallas kernels, body(): pl.pallas_call(functools.partial(block_kernel, rows, cols, channels, hidd...  60.3 us
    pallas_call x1, Pallas kernels, merged(): pl.pallas_call(functools.partial(merge_kernel, nr, nc, channels), out_sha...  26.9 us
    pallas_call x1, Pallas kernels, halo(): pl.pallas_call(functools.partial(halo_kernel, nr, nc), out_shape=[jax.Sha...  24.9 us
    unnamed x6, local copies, waits for them, and re-layouts  7.39 us

profile of v3, /device:TPU:1, one launch (start us, length us, event | category | flops | bytes accessed | tf_op | source)
XLA Modules:
  0.0 123.6 jit_solution(11792259471265718979)
XLA Ops:
  0.6 0.0 copy-start
  0.6 0.8 fusion
  1.4 0.7 pad.4.bias_ref
  2.1 1.8 %copy.20.q_raw_ref = bf16[512,192]{1,0:T(8,128)(2,1)} copy(bf16[512,192]{0,1:T(8,128)(2,1)} %param.28) | data formatting | bytes 393216 | tf_op args[13]
  3.9 1.9 %copy.19.wout_ref = bf16[768,192]{1,0:T(8,128)(2,1)} copy(bf16[768,192]{0,1:T(8,128)(2,1)} %param.23) | data formatting | bytes 589824 | tf_op args[8]
  5.8 3.7 %copy.18.x_ref = bf16[16,256,192]{2,1,0:T(8,128)(2,1)} copy(bf16[16,256,192]{1,2,0:T(8,128)(2,1)} %param.15) | data formatting | bytes 3145728 | tf_op args[0]
  9.5 24.9 %halo.1 = (bf16[3,256,192]{2,1,0:T(8,128)(2,1)}, bf16[3,256,192]{2,1,0:T(8,128)(2,1)}, bf16[22,16,192]{2,1,0:T(8,128)(2,1)}, bf16[22,16,192]{2,1,0:T(8,128)(2,1)}) custom-call(bf16[16,256,192]{2,1,0:T(8,128)(2,1)} %copy.18.x_ref), custom_call_target="tpu_custom_call" | custom-call | tf_op jit(solution)/shard_map/halo/pallas_call | solution.py:424
  34.3 60.3 %block.1 = (bf16[16,192,256]{2,1,0:T(8,128)(2,1)}, f32[512,256]{1,0:T(8,128)}) custom-call(bf16[16,256,192]{2,1,0:T(8,128)(2,1)} %copy.18.x_ref, bf16[3,256,192]{2,1,0:T(8,128)(2,1)} %get-tuple-element.8.above_ref, bf16[3,256,192]{2,1,0:T(8,128)(2,1)} %get-tuple-element.9.below_ref, bf16[22,16,192]{2,1,0:T(8,128)(2,1)} %get-tuple-element.10.left_ref, ...), custom_call_target="tpu_custom_call" | custom-call | tf_op jit(solution)/shard_map/block/pallas_call | solution.py:463
  94.7 26.9 %merge.1 = bf16[4,8,16,192]{3,2,1,0:T(8,128)(2,1)} custom-call(f32[4,128,256]{2,1,0:T(8,128)} %bitcast.10), custom_call_target="tpu_custom_call" | custom-call | tf_op jit(solution)/shard_map/merge/pallas_call | solution.py:312
  121.6 0.0 copy-done
  121.6 1.9 %fusion.1 = f32[512,192]{0,1:T(8,128)} fusion(bf16[512,192]{1,0:T(8,128)(2,1)} %bitcast.9, bf16[192,192]{1,0:T(8,128)(2,1)S(1)} %copy-done), kind=kOutput, calls=%fused_computation.2 | convolution fusion | flops 37748736 | bytes 663552 | tf_op jit(solution)/shard_map/dot_general | solution.py:504
  (1 shorter events, 0.0 us)
Async XLA Ops:
  0.6 121.0 %copy-start = (bf16[192,192]{1,0:T(8,128)(2,1)S(1)}, bf16[192,192]{1,0:T(8,128)(2,1)}, u32[]{:S(2)}) copy-start(bf16[192,192]{1,0:T(8,128)(2,1)} %param.29) | copy-start | bytes 221188

commit v4 on v3

--- a/solution.py
+++ b/solution.py
@@ -23,6 +23,8 @@
     x_ref,
     above_ref,
     below_ref,
+    above_high_ref,
+    below_high_ref,
     left_ref,
     right_ref,
     bias_ref,
@@ -72,9 +74,16 @@
 
     lax.fori_loop(0, rows, widen, 0)
     lax.fori_loop(0, rows + 6, sides, 0)
+    half_cols = cols // 2
     for i in range(3):
-        place(i, PAD, cols, above_ref[i])
-        place(rows + 3 + i, PAD, cols, below_ref[i])
+        for base, low_ref, high_ref in (
+            (0, above_ref, above_high_ref),
+            (rows + 3, below_ref, below_high_ref),
+        ):
+            xf_ref[0, base + i, PAD : PAD + cols] = low_ref[i].astype(jnp.float32)
+            line = high_ref[i].astype(jnp.float32)
+            xf_ref[1, base + i, PAD : PAD + half_cols, 0:high] = line[:, 0:high]
+            xf_ref[1, base + i, PAD + half_cols : PAD + cols, 0:high] = line[:, high : 2 * high]
     for i in range(7):
         for j in range(7):
             dw_ref[0, i, j] = jnp.broadcast_to(dw_raw_ref[i, j : j + 1, 0:128], (8, 128))
@@ -336,17 +345,25 @@
     x_ref,
     above_out,
     below_out,
+    above_high_out,
+    below_high_out,
     left_out,
     right_out,
     above,
     below,
+    above_high,
+    below_high,
     left,
     right,
+    packed,
     send,
     recv,
+    send_high,
+    recv_high,
 ):
     r, c = lax.axis_index("row"), lax.axis_index("col")
-    rows, cols = x_ref.shape[0], x_ref.shape[1]
+    rows, cols, channels = x_ref.shape
+    high, half_cols = channels - 128, cols // 2
 
     def inside(dr, dc):
         return (r + dr >= 0) & (r + dr < nr) & (c + dc >= 0) & (c + dc < nc)
@@ -361,11 +378,18 @@
         def _(dr=dr, dc=dc):
             pl.semaphore_signal(barrier, inc=1, device_id=(r + dr, c + dc), device_id_type=MESH)
 
+    for i in range(3):
+        for edge, row in ((0, i), (1, rows - 3 + i)):
+            line = x_ref[row, :, 128:channels]
+            packed[edge, i, :, 0:high] = line[0:half_cols]
+            packed[edge, i, :, high : 2 * high] = line[half_cols:cols]
     pl.semaphore_wait(barrier, count)
 
     def source(dr, dc):
         at = {-1: pl.ds(0, 3), 0: pl.ds(0, rows), 1: pl.ds(rows - 3, 3)}[dr]
         to = {-1: pl.ds(0, PAD), 0: pl.ds(0, cols), 1: pl.ds(cols - PAD, PAD)}[dc]
+        if dc == 0:
+            return x_ref.at[at, to, pl.ds(0, 128)]
         return x_ref.at[at, to]
 
     def target(dr, dc):
@@ -386,11 +410,24 @@
             device_id_type=MESH,
         )
 
+    def copy_high(d):
+        dr, dc = SIDES[d]
+        return pltpu.make_async_remote_copy(
+            src_ref=packed.at[0 if dr < 0 else 1],
+            dst_ref=below_high if dr < 0 else above_high,
+            send_sem=send_high.at[d],
+            recv_sem=recv_high.at[d],
+            device_id=(r + dr, c + dc),
+            device_id_type=MESH,
+        )
+
     for d, (dr, dc) in enumerate(SIDES):
 
         @pl.when(inside(dr, dc))
-        def _(d=d):
+        def _(d=d, dc=dc):
             copy(d).start()
+            if dc == 0:
+                copy_high(d).start()
 
     for d, (dr, dc) in enumerate(SIDES):
 
@@ -398,36 +435,48 @@
         def _(dr=dr, dc=dc):
             place = target(dr, dc)
             place[...] = jnp.zeros(place.shape, place.dtype)
+            if dc == 0:
+                other = below_high if dr < 0 else above_high
+                other[...] = jnp.zeros(other.shape, other.dtype)
 
     for d, (dr, dc) in enumerate(SIDES):
 
         @pl.when(inside(-dr, -dc))
-        def _(d=d):
+        def _(d=d, dc=dc):
             copy(d).wait_recv()
+            if dc == 0:
+                copy_high(d).wait_recv()
 
     above_out[...] = above[...]
     below_out[...] = below[...]
+    above_high_out[...] = above_high[...]
+    below_high_out[...] = below_high[...]
     left_out[...] = left[...]
     right_out[...] = right[...]
     for d, (dr, dc) in enumerate(SIDES):
 
         @pl.when(inside(dr, dc))
-        def _(d=d):
+        def _(d=d, dc=dc):
             copy(d).wait_send()
+            if dc == 0:
+                copy_high(d).wait_send()
 
 
 def halo(feature):
     nr, nc = lax.axis_size("row"), lax.axis_size("col")
     rows, cols, channels = feature.shape
     whole = pl.BlockSpec(memory_space=pltpu.VMEM)
-    shapes = [(3, cols, channels)] * 2 + [(rows + 6, PAD, channels)] * 2
+    high_shape = (3, cols // 2, 2 * (channels - 128))
+    shapes = [(3, cols, 128)] * 2 + [high_shape] * 2 + [(rows + 6, PAD, channels)] * 2
     return pl.pallas_call(
         functools.partial(halo_kernel, nr, nc),
         out_shape=[jax.ShapeDtypeStruct(shape, feature.dtype) for shape in shapes],
         in_specs=[whole],
-        out_specs=[whole] * 4,
+        out_specs=[whole] * 6,
         scratch_shapes=[pltpu.VMEM(shape, feature.dtype) for shape in shapes]
-        + [pltpu.SemaphoreType.DMA((8,)), pltpu.SemaphoreType.DMA((8,))],
+        + [pltpu.VMEM((2,) + high_shape, feature.dtype)]
+        + [pltpu.SemaphoreType.DMA((8,))] * 2
+        + [pltpu.SemaphoreType.DMA((2,))] * 2,
         compiler_params=pltpu.CompilerParams(collective_id=1, has_side_effects=True),
         name="halo",
     )(feature)
@@ -455,7 +504,7 @@
     hidden = w_in.shape[1]
     query_count = queries.shape[0]
     depth = channels + 16
-    above, below, left, right = halo(feature)
+    strips = halo(feature)
     bias = jnp.where(mask > 0, 0.0, MASKED).astype(jnp.bfloat16).reshape(1, positions)
     bias = jnp.pad(bias, ((0, 15), (0, 0)))
     qb = 256
@@ -466,7 +515,7 @@
             jax.ShapeDtypeStruct((rows, channels, cols), jnp.bfloat16),
             jax.ShapeDtypeStruct((query_count, 256), jnp.float32),
         ),
-        in_specs=[whole] * 18,
+        in_specs=[whole] * 20,
         out_specs=(whole, whole),
         scratch_shapes=[
             pltpu.VMEM((2, 7, 7, 8, 128), jnp.float32),
@@ -483,10 +532,7 @@
         name="block",
     )(
         feature,
-        above,
-        below,
-        left,
-        right,
+        *strips,
         bias,
         dw_weight,
         dw_bias,

time: 124 us -> 120 us (0.968)
  Pallas kernels: 112 us -> 108 us
    pallas_call x1, Pallas kernels: 24.9 us -> 20.6 us  [halo(): pl.pallas_call(functools.partial(halo_kernel, nr, nc), out_shape=[jax.Sha...]
where the time goes in v4:
time: 120 us; the launch traced here: 119 us
  Pallas kernels  108 us (90%)
  local copies, waits for them, and re-layouts  8.05 us (7%)
  matrix products  1.95 us (2%)
    pallas_call x1, Pallas kernels, body(): pl.pallas_call(functools.partial(block_kernel, rows, cols, channels, hidd...  60.3 us
    pallas_call x1, Pallas kernels, merged(): pl.pallas_call(functools.partial(merge_kernel, nr, nc, channels), out_sha...  26.9 us
    pallas_call x1, Pallas kernels, halo(): pl.pallas_call(functools.partial(halo_kernel, nr, nc), out_shape=[jax.Sha...  20.6 us
    unnamed x6, local copies, waits for them, and re-layouts  7.38 us

profile of v4, /device:TPU:1, one launch (start us, length us, event | category | flops | bytes accessed | tf_op | source)
XLA Modules:
  0.0 119.3 jit_solution(11572170295826133990)
XLA Ops:
  0.6 0.0 copy-start
  0.6 0.8 fusion
  1.4 0.7 pad.4.bias_ref
  2.1 1.8 %copy.20.q_raw_ref = bf16[512,192]{1,0:T(8,128)(2,1)} copy(bf16[512,192]{0,1:T(8,128)(2,1)} %param.28) | data formatting | bytes 393216 | tf_op args[13]
  3.9 1.9 %copy.19.wout_ref = bf16[768,192]{1,0:T(8,128)(2,1)} copy(bf16[768,192]{0,1:T(8,128)(2,1)} %param.23) | data formatting | bytes 589824 | tf_op args[8]
  5.7 3.7 %copy.18.x_ref = bf16[16,256,192]{2,1,0:T(8,128)(2,1)} copy(bf16[16,256,192]{1,2,0:T(8,128)(2,1)} %param.15) | data formatting | bytes 3145728 | tf_op args[0]
  9.5 20.6 %halo.1 = (bf16[3,256,128]{2,1,0:T(8,128)(2,1)}, bf16[3,256,128]{2,1,0:T(8,128)(2,1)}, bf16[3,128,128]{2,1,0:T(8,128)(2,1)}, bf16[3,128,128]{2,1,0:T(8,128)(2,1)...) custom-call(bf16[16,256,192]{2,1,0:T(8,128)(2,1)} %copy.18.x_ref), custom_call_target="tpu_custom_call" | custom-call | tf_op jit(solution)/shard_map/halo/pallas_call | solution.py:471
  30.1 60.3 %block.1 = (bf16[16,192,256]{2,1,0:T(8,128)(2,1)}, f32[512,256]{1,0:T(8,128)}) custom-call(bf16[16,256,192]{2,1,0:T(8,128)(2,1)} %copy.18.x_ref, bf16[3,256,128]{2,1,0:T(8,128)(2,1)} %get-tuple-element.10.above_ref, bf16[3,256,128]{2,1,0:T(8,128)(2,1)} %get-tuple-element.11.below_ref, bf16[3,128,128]{2,1,0:T(8,128)(2,1)} %get-tuple-element.12.above_high_ref, ...), custom_call_target="tpu_custom_call" | custom-call | tf_op jit(solution)/shard_map/block/pallas_call | solution.py:512
  90.4 26.9 %merge.1 = bf16[4,8,16,192]{3,2,1,0:T(8,128)(2,1)} custom-call(f32[4,128,256]{2,1,0:T(8,128)} %bitcast.10), custom_call_target="tpu_custom_call" | custom-call | tf_op jit(solution)/shard_map/merge/pallas_call | solution.py:321
  117.4 0.0 copy-done
  117.4 1.9 %fusion.1 = f32[512,192]{0,1:T(8,128)} fusion(bf16[512,192]{1,0:T(8,128)(2,1)} %bitcast.9, bf16[192,192]{1,0:T(8,128)(2,1)S(1)} %copy-done), kind=kOutput, calls=%fused_computation.2 | convolution fusion | flops 37748736 | bytes 663552 | tf_op jit(solution)/shard_map/dot_general | solution.py:550
  (1 shorter events, 0.0 us)
Async XLA Ops:
  0.6 116.7 %copy-start = (bf16[192,192]{1,0:T(8,128)(2,1)S(1)}, bf16[192,192]{1,0:T(8,128)(2,1)}, u32[]{:S(2)}) copy-start(bf16[192,192]{1,0:T(8,128)(2,1)} %param.29) | copy-start | bytes 221188

commit v5 on v4

--- a/solution.py
+++ b/solution.py
@@ -94,7 +94,7 @@
     q_lane = lax.broadcasted_iota(jnp.int32, (query_count, channels), 1) // head_size
     tail_lane = lax.broadcasted_iota(jnp.int32, (query_count, depth - channels), 1)
     q_tail = jnp.where(tail_lane == 0, 1.0, 0.0).astype(jnp.bfloat16)
-    q_all = q_raw_ref[...].astype(jnp.float32)
+    q_all = jnp.transpose(q_raw_ref[...].astype(jnp.float32))
     for head in range(NH):
         at = head * query_count
         own = jnp.where(q_lane == head, q_all, 0.0).astype(jnp.bfloat16)
@@ -142,7 +142,10 @@
         normed = (moved * lax.rsqrt(spread + 1e-06) * gain + shift).astype(jnp.bfloat16)
         inner = jnp.dot(normed, win_ref[...], preferred_element_type=jnp.float32) + b_in
         act = (0.5 * inner * (1.0 + lax.erf(inner * math.sqrt(0.5)))).astype(jnp.bfloat16)
-        branch = jnp.dot(act, wout_ref[...], preferred_element_type=jnp.float32) + b_out
+        branch = lax.dot_general(
+            act, wout_ref[...], (((1,), (1,)), ((), ())), preferred_element_type=jnp.float32
+        )
+        branch = branch + b_out
         summed = center.astype(jnp.float32) + scale * branch
         result = summed.astype(jnp.bfloat16)
         for i in range(2):
@@ -542,10 +545,10 @@
         layer_scale,
         w_in,
         b_in,
-        w_out,
+        jnp.transpose(w_out),
         w_key,
         w_value,
-        queries,
+        jnp.transpose(queries),
     )
     pooled_out = jnp.dot(
         merged(part, channels), w_proj, preferred_element_type=jnp.float32

time: 120 us -> 116 us (0.967)
  local copies, waits for them, and re-layouts: 8.05 us -> 4.4 us
    unnamed x6 -> x4, local copies, waits for them, and re-layouts: 7.38 us -> 3.73 us
where the time goes in v5:
time: 116 us
  Pallas kernels  108 us (93%)
  local copies, waits for them, and re-layouts  4.4 us (4%)
  matrix products  1.95 us (2%)
    pallas_call x1, Pallas kernels, body(): pl.pallas_call(functools.partial(block_kernel, rows, cols, channels, hidd...  60.3 us
    pallas_call x1, Pallas kernels, merged(): pl.pallas_call(functools.partial(merge_kernel, nr, nc, channels), out_sha...  26.9 us
    pallas_call x1, Pallas kernels, halo(): pl.pallas_call(functools.partial(halo_kernel, nr, nc), out_shape=[jax.Sha...  20.7 us
    unnamed x4, local copies, waits for them, and re-layouts  3.73 us

profile of v5, /device:TPU:1, one launch (start us, length us, event | category | flops | bytes accessed | tf_op | source)
XLA Modules:
  0.0 115.7 jit_solution(1873855775775611642)
XLA Ops:
  0.6 0.0 copy-start
  0.6 0.8 fusion
  1.4 0.7 pad.4.bias_ref
  2.1 3.7 %copy.18.x_ref = bf16[16,256,192]{2,1,0:T(8,128)(2,1)} copy(bf16[16,256,192]{1,2,0:T(8,128)(2,1)} %param.15) | data formatting | bytes 3145728 | tf_op args[0]
  5.8 20.7 %halo.1 = (bf16[3,256,128]{2,1,0:T(8,128)(2,1)}, bf16[3,256,128]{2,1,0:T(8,128)(2,1)}, bf16[3,128,128]{2,1,0:T(8,128)(2,1)}, bf16[3,128,128]{2,1,0:T(8,128)(2,1)...) custom-call(bf16[16,256,192]{2,1,0:T(8,128)(2,1)} %copy.18.x_ref), custom_call_target="tpu_custom_call" | custom-call | tf_op jit(solution)/shard_map/halo/pallas_call | solution.py:474
  26.5 60.3 %block.1 = (bf16[16,192,256]{2,1,0:T(8,128)(2,1)}, f32[512,256]{1,0:T(8,128)}) custom-call(bf16[16,256,192]{2,1,0:T(8,128)(2,1)} %copy.18.x_ref, bf16[3,256,128]{2,1,0:T(8,128)(2,1)} %get-tuple-element.10.above_ref, bf16[3,256,128]{2,1,0:T(8,128)(2,1)} %get-tuple-element.11.below_ref, bf16[3,128,128]{2,1,0:T(8,128)(2,1)} %get-tuple-element.12.above_high_ref, ...), custom_call_target="tpu_custom_call" | custom-call | tf_op jit(solution)/shard_map/block/pallas_call | solution.py:515
  86.8 26.9 %merge.1 = bf16[4,8,16,192]{3,2,1,0:T(8,128)(2,1)} custom-call(f32[4,128,256]{2,1,0:T(8,128)} %bitcast.12), custom_call_target="tpu_custom_call" | custom-call | tf_op jit(solution)/shard_map/merge/pallas_call | solution.py:324
  113.8 0.0 copy-done
  113.8 1.9 %fusion.1 = f32[512,192]{0,1:T(8,128)} fusion(bf16[512,192]{1,0:T(8,128)(2,1)} %bitcast.11, bf16[192,192]{1,0:T(8,128)(2,1)S(1)} %copy-done), kind=kOutput, calls=%fused_computation.2 | convolution fusion | flops 37748736 | bytes 663552 | tf_op jit(solution)/shard_map/dot_general | solution.py:553
  (1 shorter events, 0.0 us)
Async XLA Ops:
  0.6 113.2 %copy-start = (bf16[192,192]{1,0:T(8,128)(2,1)S(1)}, bf16[192,192]{1,0:T(8,128)(2,1)}, u32[]{:S(2)}) copy-start(bf16[192,192]{1,0:T(8,128)(2,1)} %param.29) | copy-start | bytes 221188
